TPU v7x, 256 devices: a whole 4x4x8 slice. The times are simulated.
256 devices in a mesh: trade: 16 (over x_hi, y, core), scen: 16 (over x_lo, z).
Axes of the slice: x: 4 (x_hi: 2, x_lo: 2; x = x_hi * 2 + x_lo), y: 4, z: 8, core: 2. Of those that a mesh axis runs over, the one named last changes fastest.
Arguments:
- loadings: bfloat16 [200, 512, 1024], P(None, ('trade', 'scen')), may hold values from -0.4375 to 0.4375
- base_coef: bfloat16 [512, 1024], P(('trade', 'scen')), may hold values from -3 to 3
- shocks: float32 [32, 200], P('scen'), may hold values from -6 to 6
- scen_class: int32 [32], P('scen'), may hold values from 0 to 4, as said below
- names: int32 [256, 2], P('trade'), may hold values from 0 to 511, as said below
- trade_kind: int32 [256], P('trade'), may hold values from 0 to 1
- call_start: int32 [256], P('trade'), may hold values from 8 to 39
- knock_start: int32 [256], P('trade'), may hold values from 0 to 31
- offsets: int32 [256], P('trade'), may hold values from 0 to 2047
- normal_table: float32 [64, 2048], replicated, may hold values from -5 to 5
- book_value: float32 [256], P('trade'), may hold values from 0.5 to 1.5
Outputs:
- trade_value: float32 [256, 32], P('trade', 'scen')
- desk_pnl: float32 [32], P('scen')
- shortfall: float32 [], replicated
Inputs may be any that keep to these rules, and one draw needn't show every extreme that they name: names = owner * 32 + local with owner the index of trade that holds the underlying. The trades of one index of trade (rows t * 16 to (t + 1) * 16 - 1) name underlyings of one owner at most 4 times over both columns, and exactly 4 times for some owner. The two names of a trade differ. scen_class[s] differs from (5 s) // 32 by at most one; scenario 0 has class 0.
All inputs are finite; a program needn't handle non-finite values.
Results may differ from a plain program's by a relative error of at most 0.0003.
Values may be sent and summed in bfloat16 or wider, within the bound.
No kernel may reach another device: no remote copies, remote signals or barrier semaphores. Data moves between devices by JAX's collectives and lax.ppermute only.
A program may use at most 64 MiB of HBM per device.

v0:
```python
import math

import jax
import jax.numpy as jnp
from jax import lax
from jax.sharding import PartitionSpec as P

MAT = 64
COEF = 16
TROWS = 2048
PATHS = 256
ES_TAIL = 4


CORRELATION = 0.6
CORR_COMPLEMENT = 0.8
BARRIER_LOG = -0.35
SMOOTHING = 0.03
COUPON_RATE = 0.08


def joined_along(pieces, dim):
    pieces = jnp.moveaxis(pieces, 0, dim)
    lengths = pieces.shape
    return pieces.reshape(*lengths[:dim], lengths[dim] * lengths[dim + 1], *lengths[dim + 2 :])


def copy_for_each(array, axis):
    copies = jnp.broadcast_to(array, (lax.axis_size(axis), *array.shape))
    return lax.all_to_all(copies, axis, split_axis=0, concat_axis=0, tiled=True)


def gather_directly(array, axis, dim):
    return joined_along(copy_for_each(array, axis), dim)


def of_everyone(array, axis):
    return copy_for_each(array, axis).sum(axis=0)


def combined_pairwise(pieces, combine):
    while len(jax.tree.leaves(pieces)[0]) > 1:
        pieces = jax.vmap(combine)(*(pieces[side::2] for side in (0, 1)))
    return pieces[0]


def joined_all(array, axis, combine):
    pieces = copy_for_each(array, axis)
    return combined_pairwise(pieces, combine)


def local_vol(coefficients, log_level):
    bent = jnp.tanh(log_level)
    cheb_prev = jnp.ones_like(bent)
    cheb_now = bent
    argument = (
        coefficients[..., 0][..., None] * cheb_prev + coefficients[..., 1][..., None] * cheb_now
    )
    for degree in range(2, coefficients.shape[-1]):
        cheb_next = 2.0 * bent * cheb_now - cheb_prev
        argument = argument + coefficients[..., degree][..., None] * cheb_next
        cheb_prev, cheb_now = (cheb_now, cheb_next)
    return 0.05 + 0.45 * jax.nn.sigmoid(argument)


def advance(
    path_state,
    step_index,
    draw_first,
    draw_other,
    coef_first,
    coef_second,
    call_start,
    knock_start,
    steps,
):
    logs_first, logs_second, survival, alive_share, paid_value = path_state
    step_size = 1.0 / steps
    root_step = math.sqrt(step_size)
    vol_first = local_vol(coef_first, logs_first)
    vol_second = local_vol(coef_second, logs_second)
    shock_first = draw_first[:, None, :]
    shock_second = (CORRELATION * draw_first + CORR_COMPLEMENT * draw_other)[:, None, :]
    logs_first = (
        logs_first - 0.5 * vol_first * vol_first * step_size + vol_first * root_step * shock_first
    )
    logs_second = (
        logs_second
        - 0.5 * vol_second * vol_second * step_size
        + vol_second * root_step * shock_second
    )
    worst_log = jnp.minimum(logs_first, logs_second)
    watched = (step_index >= knock_start)[:, None, None]
    survival = jnp.where(
        watched, survival * (1.0 - jax.nn.sigmoid((BARRIER_LOG - worst_log) / SMOOTHING)), survival
    )
    call_gap = steps // 8
    observed = (
        (step_index >= call_start)
        & ((step_index - call_start) % call_gap == 0)
        & (step_index < steps - 1)
    )[:, None, None]
    call_prob = jax.nn.sigmoid(worst_log / SMOOTHING)
    coupon = 1.0 + COUPON_RATE * (step_index + 1).astype(jnp.float32) / steps
    paid_value = jnp.where(observed, paid_value + alive_share * call_prob * coupon, paid_value)
    alive_share = jnp.where(observed, alive_share * (1.0 - call_prob), alive_share)
    return (logs_first, logs_second, survival, alive_share, paid_value)


def settle(path_state, trade_kind):
    logs_first, logs_second, survival, alive_share, paid_value = path_state
    worst_log = jnp.minimum(logs_first, logs_second)
    knocked = 1.0 - survival
    growth = jnp.exp(worst_log)
    note_value = paid_value + alive_share * (1.0 + knocked * jnp.minimum(growth - 1.0, 0.0))
    put_value = knocked * jnp.maximum(1.0 - growth, 0.0)
    payoff = jnp.where((trade_kind == 0)[:, None, None], note_value, put_value)
    return jnp.mean(payoff, axis=-1)


def horizon_scale(class_ids):
    table = jnp.sqrt(jnp.array([1.0, 2.0, 4.0, 6.0, 12.0], jnp.float32))
    hits = class_ids[:, None] == jnp.arange(5, dtype=jnp.int32)[None, :]
    return jnp.sum(jnp.where(hits, table[None, :], 0.0), axis=1)


def keep_worst(first_set, second_set):
    return lax.top_k(jnp.concatenate([first_set, second_set]), first_set.shape[0])[0]


def per_device(
    loadings,
    base_coef,
    shocks,
    scen_class,
    names,
    trade_kind,
    call_start,
    knock_start,
    offsets,
    normal_table,
    book_value,
):
    factors = shocks.shape[1]
    scen_here = shocks.shape[0]
    trades_here = names.shape[0]
    bucket = jnp.arange(factors, dtype=jnp.int32) * 5 // factors
    masked = jnp.where(bucket[None, :] >= scen_class[:, None], shocks, 0.0).astype(jnp.bfloat16)
    everyone = gather_directly(masked, "scen", 0)
    product = jnp.einsum("sf,fum->usm", everyone, loadings, preferred_element_type=jnp.float32)
    own_coef = (product + base_coef[:, None, :].astype(jnp.float32)).astype(jnp.bfloat16)
    owned = lax.all_to_all(own_coef, "scen", split_axis=1, concat_axis=0, tiled=True)
    owned_rows = owned.shape[0]
    row_width = owned.shape[1] * owned.shape[2]
    coef_rows = owned.reshape(owned_rows, row_width)
    leg_names = names.reshape(-1)
    leg_total = leg_names.shape[0]
    width_trade = lax.axis_size("trade")
    cap_slots = max(2, (4 * trades_here + width_trade - 1) // width_trade)
    owner_row = leg_names // owned_rows
    local_row = leg_names % owned_rows
    leg_ids = jnp.arange(leg_total, dtype=jnp.int32)
    same_owner = (owner_row[None, :] == owner_row[:, None]) & (leg_ids[None, :] < leg_ids[:, None])
    slot_rank = jnp.sum(same_owner.astype(jnp.int32), axis=1)
    owner_match = (
        owner_row[None, None, :] == jnp.arange(width_trade, dtype=jnp.int32)[:, None, None]
    )
    slot_match = slot_rank[None, None, :] == jnp.arange(cap_slots, dtype=jnp.int32)[None, :, None]
    wanted_rows = jnp.sum(jnp.where(owner_match & slot_match, local_row[None, None, :], 0), axis=2)
    fetched = coef_rows[
        lax.all_to_all(wanted_rows, "trade", split_axis=0, concat_axis=0, tiled=True)
    ]
    replies = lax.all_to_all(fetched, "trade", split_axis=0, concat_axis=0, tiled=True)
    leg_rows = replies[owner_row, slot_rank]
    leg_coef = leg_rows.reshape(trades_here, 2, scen_here, MAT, COEF)
    coef_first = leg_coef[:, 0].astype(jnp.float32).transpose(2, 0, 1, 3)
    coef_second = leg_coef[:, 1].astype(jnp.float32).transpose(2, 0, 1, 3)
    row_index = (offsets[:, None] + jnp.arange(PATHS, dtype=jnp.int32)[None, :]) % TROWS
    draw_first = normal_table[:, row_index]
    draw_other = normal_table[:, (row_index + TROWS // 2) % TROWS]
    block_total = MAT // 8
    zeros = jnp.zeros((trades_here, scen_here, PATHS), jnp.float32)
    ones = jnp.ones((trades_here, scen_here, PATHS), jnp.float32)
    start_state = (zeros, zeros, ones, ones, zeros)

    def run_block(path_state, inputs):
        block_index, first_block, other_block, coef_a, coef_b = inputs
        for inner in range(8):
            path_state = advance(
                path_state,
                block_index * 8 + inner,
                first_block[inner],
                other_block[inner],
                coef_a[inner],
                coef_b[inner],
                call_start,
                knock_start,
                MAT,
            )
        return (path_state, None)

    block_inputs = (
        jnp.arange(block_total, dtype=jnp.int32),
        draw_first.reshape(block_total, 8, trades_here, PATHS),
        draw_other.reshape(block_total, 8, trades_here, PATHS),
        coef_first.reshape(block_total, 8, trades_here, scen_here, COEF),
        coef_second.reshape(block_total, 8, trades_here, scen_here, COEF),
    )
    final_state, _ = lax.scan(run_block, start_state, block_inputs)
    trade_value = settle(final_state, trade_kind)
    partial_pnl = jnp.sum(trade_value - book_value[:, None], axis=0)
    total_pnl = of_everyone(partial_pnl, "trade")
    desk_pnl = total_pnl / math.sqrt(trades_here * lax.axis_size("trade"))
    losses = -desk_pnl * horizon_scale(scen_class)
    candidates = jnp.concatenate([losses, jnp.full((ES_TAIL,), -1e30, jnp.float32)])
    local_tail = lax.top_k(candidates, ES_TAIL)[0]
    merged_tail = joined_all(local_tail, "scen", keep_worst)
    shortfall = jnp.mean(merged_tail)
    return (trade_value, desk_pnl, shortfall)


def solution(mesh):
    return jax.shard_map(
        per_device,
        mesh=mesh,
        in_specs=(
            P(None, ("trade", "scen"), None),
            P(("trade", "scen"), None),
            P("scen", None),
            P("scen"),
            P("trade", None),
            P("trade"),
            P("trade"),
            P("trade"),
            P("trade"),
            P(),
            P("trade"),
        ),
        out_specs=(P("trade", "scen"), P("scen"), P()),
        check_vma=False,
    )
```

profile of v0, /device:TPU:1, one launch (start us, length us, event | category | flops | bytes accessed | tf_op | source)
XLA Modules:
  0.0 299.4 jit_solution(16107255821230783536)
XLA Ops:
  2.6 8.4 %all-to-all-start.2 = ((s32[16,1,4]{2,1,0:T(1,128)}), s32[16,1,4]{2,1,0:T(1,128)S(1)}, u32[]{:S(2)}, u32[]{:S(2)}) async-start(s32[16,1,4]{2,1,0:T(1,128)} %copy.1376), calls=%async_computation.2 | async-start | bytes 16384 | tf_op jit(solution)/shard_map/all_to_all | solution.py:171
  12.6 5.4 %all-to-all-done.2 = s32[16,1,4]{2,1,0:T(1,128)S(1)} async-done(((s32[16,1,4]{2,1,0:T(1,128)}), s32[16,1,4]{2,1,0:T(1,128)S(1)}, u32[]{:S(2)}, u32[]{:S(2)}) %all-to-all-start.2) | async-done | bytes 288 | tf_op jit(solution)/shard_map/all_to_all | solution.py:171
  18.7 8.3 %all-to-all-start = ((bf16[16,2,200]{2,1,0:T(2,128)(2,1)}), bf16[16,2,200]{2,1,0:T(2,128)(2,1)S(1)}, u32[]{:S(2)}, u32[]{:S(2)}) async-start(bf16[16,2,200]{2,1,0:T(2,128)(2,1)} %broadcast_in_dim.279), calls=%async_computation | async-start | bytes 32768 | tf_op jit(solution)/shard_map/all_to_all | solution.py:30
  27.8 6.5 %all-to-all-done = bf16[16,2,200]{2,1,0:T(2,128)(2,1)S(1)} async-done(((bf16[16,2,200]{2,1,0:T(2,128)(2,1)}), bf16[16,2,200]{2,1,0:T(2,128)(2,1)S(1)}, u32[]{:S(2)}, u32[]{:S(2)}) %all-to-all-start) | async-done | bytes 12832 | tf_op jit(solution)/shard_map/all_to_all | solution.py:30
  35.5 3.6 %all-to-all-start.1 = ((bf16[2,32,1024]{2,0,1:T(2,128)(2,1)}), bf16[2,32,1024]{2,0,1:T(2,128)(2,1)S(1)}, u32[]{:S(2)}, u32[]{:S(2)}) async-start(bf16[2,32,1024]{2,0,1:T(2,128)(2,1)} %copy.1373), calls=%async_computation.1 | async-start | bytes 262144 | tf_op jit(solution)/shard_map/all_to_all | solution.py:152
  39.4 7.3 %all-to-all-done.1 = bf16[2,32,1024]{2,0,1:T(2,128)(2,1)S(1)} async-done(((bf16[2,32,1024]{2,0,1:T(2,128)(2,1)}), bf16[2,32,1024]{2,0,1:T(2,128)(2,1)S(1)}, u32[]{:S(2)}, u32[]{:S(2)}) %all-to-all-start.1) | async-done | bytes 131104 | tf_op jit(solution)/shard_map/all_to_all | solution.py:152
  48.3 6.4 %all-to-all-start.3 = ((bf16[16,4,2048]{2,1,0:T(4,128)(2,1)}), bf16[16,4,2048]{2,1,0:T(4,128)(2,1)S(1)}, u32[]{:S(2)}, u32[]{:S(2)}) async-start(bf16[16,4,2048]{2,1,0:T(4,128)(2,1)} %reshape.929), calls=%async_computation.3 | async-start | bytes 524288 | tf_op jit(solution)/shard_map/all_to_all | solution.py:173
  55.2 14.1 %gather_fusion.2 = f32[4096,64]{1,0:T(8,128)} fusion(f32[64,2048]{0,1:T(8,128)S(1)} %copy.1380, s32[4096]{0:T(1024)S(1)} %broadcast_clamp_fusion.1), kind=kCustom, calls=%fused_computation.2 | custom fusion | bytes 2113536 | tf_op jit(solution)/shard_map/gather | solution.py:179
  69.3 2.5 copy.1381
  71.8 14.1 %gather_fusion.3 = f32[4096,64]{1,0:T(8,128)} fusion(f32[64,2048]{0,1:T(8,128)S(1)} %copy.1380, s32[4096]{0:T(1024)S(1)} %broadcast_clamp_fusion), kind=kCustom, calls=%fused_computation.3 | custom fusion | bytes 2113536 | tf_op jit(solution)/shard_map/gather | solution.py:180
  85.9 3.4 %copy.1383 = f32[64,16,256]{2,1,0:T(8,128)} copy(f32[64,16,256]{0,2,1:T(8,128)} %bitcast.685) | data formatting | bytes 2097152 | tf_op jit(solution)/shard_map/gather | solution.py:180
  92.8 172.7 %while.22 = (s32[]{:T(128)}, f32[16,2,256]{2,0,1:T(8,128)S(1)}, f32[16,2,256]{2,0,1:T(8,128)S(1)}, f32[16,2,256]{2,0,1:T(8,128)S(1)}, f32[16,2,256]{2,0,1:T(8,12...) while((s32[]{:T(128)}, f32[16,2,256]{2,0,1:T(8,128)S(1)}, ...), condition=%wide.region_3.4_spmd.clone, body=%wide.region_2.3_spmd.clone.sunk | while | flops 31377560 | bytes 2481862 | solution.py:209
  92.8 2.6 constant_dynamic-slice_fusion.17
  100.1 5.0 %multiply_select_fusion.18 = (f32[16,2,256]{2,0,1:T(8,128)S(1)}, f32[16,2,256]{2,0,1:T(8,128)S(1)}) fusion(f32[16,2,256]{2,0,1:T(8,128)S(1)} %get-tuple-element.1479, pred[16]{0:T(512)(128)(4,1)S(1)} %get-tuple-element.1137, pred[16]{0:T(512)(128)(4,1)S(1)} %get-tuple-element.1138, pred[16]{0:T(512)(128)(4,1)S(1)} %get-tuple-element.1139, ...), kind=kLoop, calls=%fused_computation.20.clone.1 | loop fusion | flops 9216000 | bytes 473217 | tf_op jit(solution)/shard_map/while/body/eval_jaxpr/jit(_where)/select_n | solution.py:94
  105.2 4.6 %add_select_fusion.11 = f32[16,2,256]{2,0,1:T(8,128)S(1)} fusion(f32[16,2,256]{2,0,1:T(8,128)S(1)} %get-tuple-element.1481, f32[16,2,256]{2,0,1:T(8,128)S(1)} %get-tuple-element.1480, f32[]{:T(128)S(6)} %add.8789, f32[]{:T(128)S(6)} %add.8790, f32[]{:T(128)S(6)} %add.8791, f32[]{:T(128)S(6)} %add.8792, f32[]{:T(128)S(6)} %add.8793, f32[]{:T(128)S(6)} %add.8794, ...), kind=kLoop, calls=%fused_computation.4.clone.1 | loop fusion | flops 8822784 | bytes 487585 | tf_op jit(solution)/shard_map/while/body/eval_jaxpr/jit(_where)/select_n | solution.py:105
  109.8 4.6 %multiply_select_fusion.19 = f32[16,2,256]{2,0,1:T(8,128)S(1)} fusion(f32[16,2,256]{2,0,1:T(8,128)S(1)} %get-tuple-element.1480, pred[16]{0:T(512)(128)(4,1)S(1)} %get-tuple-element.1435, pred[16]{0:T(512)(128)(4,1)S(1)} %get-tuple-element.1436, pred[16]{0:T(512)(128)(4,1)S(1)} %get-tuple-element.1437, pred[16]{0:T(512)(128)(4,1)S(1)} %get-tuple-element.1438, ...), kind=kLoop, calls=%fused_computation.12.clone.1 | loop fusion | flops 8577024 | bytes 454785 | tf_op jit(solution)/shard_map/while/body/eval_jaxpr/jit(_where)/select_n | solution.py:106
  114.5 2.6 constant_dynamic-slice_fusion.17
  121.8 5.0 %multiply_select_fusion.18 = (f32[16,2,256]{2,0,1:T(8,128)S(1)}, f32[16,2,256]{2,0,1:T(8,128)S(1)}) fusion(f32[16,2,256]{2,0,1:T(8,128)S(1)} %get-tuple-element.1479, pred[16]{0:T(512)(128)(4,1)S(1)} %get-tuple-element.1137, pred[16]{0:T(512)(128)(4,1)S(1)} %get-tuple-element.1138, pred[16]{0:T(512)(128)(4,1)S(1)} %get-tuple-element.1139, ...), kind=kLoop, calls=%fused_computation.20.clone.1 | loop fusion | flops 9216000 | bytes 473217 | tf_op jit(solution)/shard_map/while/body/eval_jaxpr/jit(_where)/select_n | solution.py:94
  126.9 4.6 %add_select_fusion.11 = f32[16,2,256]{2,0,1:T(8,128)S(1)} fusion(f32[16,2,256]{2,0,1:T(8,128)S(1)} %get-tuple-element.1481, f32[16,2,256]{2,0,1:T(8,128)S(1)} %get-tuple-element.1480, f32[]{:T(128)S(6)} %add.8789, f32[]{:T(128)S(6)} %add.8790, f32[]{:T(128)S(6)} %add.8791, f32[]{:T(128)S(6)} %add.8792, f32[]{:T(128)S(6)} %add.8793, f32[]{:T(128)S(6)} %add.8794, ...), kind=kLoop, calls=%fused_computation.4.clone.1 | loop fusion | flops 8822784 | bytes 487585 | tf_op jit(solution)/shard_map/while/body/eval_jaxpr/jit(_where)/select_n | solution.py:105
  131.5 4.6 %multiply_select_fusion.19 = f32[16,2,256]{2,0,1:T(8,128)S(1)} fusion(f32[16,2,256]{2,0,1:T(8,128)S(1)} %get-tuple-element.1480, pred[16]{0:T(512)(128)(4,1)S(1)} %get-tuple-element.1435, pred[16]{0:T(512)(128)(4,1)S(1)} %get-tuple-element.1436, pred[16]{0:T(512)(128)(4,1)S(1)} %get-tuple-element.1437, pred[16]{0:T(512)(128)(4,1)S(1)} %get-tuple-element.1438, ...), kind=kLoop, calls=%fused_computation.12.clone.1 | loop fusion | flops 8577024 | bytes 454785 | tf_op jit(solution)/shard_map/while/body/eval_jaxpr/jit(_where)/select_n | solution.py:106
  136.1 2.4 constant_dynamic-slice_fusion.17
  143.2 5.0 %multiply_select_fusion.18 = (f32[16,2,256]{2,0,1:T(8,128)S(1)}, f32[16,2,256]{2,0,1:T(8,128)S(1)}) fusion(f32[16,2,256]{2,0,1:T(8,128)S(1)} %get-tuple-element.1479, pred[16]{0:T(512)(128)(4,1)S(1)} %get-tuple-element.1137, pred[16]{0:T(512)(128)(4,1)S(1)} %get-tuple-element.1138, pred[16]{0:T(512)(128)(4,1)S(1)} %get-tuple-element.1139, ...), kind=kLoop, calls=%fused_computation.20.clone.1 | loop fusion | flops 9216000 | bytes 473217 | tf_op jit(solution)/shard_map/while/body/eval_jaxpr/jit(_where)/select_n | solution.py:94
  148.3 4.6 %add_select_fusion.11 = f32[16,2,256]{2,0,1:T(8,128)S(1)} fusion(f32[16,2,256]{2,0,1:T(8,128)S(1)} %get-tuple-element.1481, f32[16,2,256]{2,0,1:T(8,128)S(1)} %get-tuple-element.1480, f32[]{:T(128)S(6)} %add.8789, f32[]{:T(128)S(6)} %add.8790, f32[]{:T(128)S(6)} %add.8791, f32[]{:T(128)S(6)} %add.8792, f32[]{:T(128)S(6)} %add.8793, f32[]{:T(128)S(6)} %add.8794, ...), kind=kLoop, calls=%fused_computation.4.clone.1 | loop fusion | flops 8822784 | bytes 487585 | tf_op jit(solution)/shard_map/while/body/eval_jaxpr/jit(_where)/select_n | solution.py:105
  152.9 4.6 %multiply_select_fusion.19 = f32[16,2,256]{2,0,1:T(8,128)S(1)} fusion(f32[16,2,256]{2,0,1:T(8,128)S(1)} %get-tuple-element.1480, pred[16]{0:T(512)(128)(4,1)S(1)} %get-tuple-element.1435, pred[16]{0:T(512)(128)(4,1)S(1)} %get-tuple-element.1436, pred[16]{0:T(512)(128)(4,1)S(1)} %get-tuple-element.1437, pred[16]{0:T(512)(128)(4,1)S(1)} %get-tuple-element.1438, ...), kind=kLoop, calls=%fused_computation.12.clone.1 | loop fusion | flops 8577024 | bytes 454785 | tf_op jit(solution)/shard_map/while/body/eval_jaxpr/jit(_where)/select_n | solution.py:106
  157.6 2.6 constant_dynamic-slice_fusion.17
  164.9 5.0 %multiply_select_fusion.18 = (f32[16,2,256]{2,0,1:T(8,128)S(1)}, f32[16,2,256]{2,0,1:T(8,128)S(1)}) fusion(f32[16,2,256]{2,0,1:T(8,128)S(1)} %get-tuple-element.1479, pred[16]{0:T(512)(128)(4,1)S(1)} %get-tuple-element.1137, pred[16]{0:T(512)(128)(4,1)S(1)} %get-tuple-element.1138, pred[16]{0:T(512)(128)(4,1)S(1)} %get-tuple-element.1139, ...), kind=kLoop, calls=%fused_computation.20.clone.1 | loop fusion | flops 9216000 | bytes 473217 | tf_op jit(solution)/shard_map/while/body/eval_jaxpr/jit(_where)/select_n | solution.py:94
  170.0 4.6 %add_select_fusion.11 = f32[16,2,256]{2,0,1:T(8,128)S(1)} fusion(f32[16,2,256]{2,0,1:T(8,128)S(1)} %get-tuple-element.1481, f32[16,2,256]{2,0,1:T(8,128)S(1)} %get-tuple-element.1480, f32[]{:T(128)S(6)} %add.8789, f32[]{:T(128)S(6)} %add.8790, f32[]{:T(128)S(6)} %add.8791, f32[]{:T(128)S(6)} %add.8792, f32[]{:T(128)S(6)} %add.8793, f32[]{:T(128)S(6)} %add.8794, ...), kind=kLoop, calls=%fused_computation.4.clone.1 | loop fusion | flops 8822784 | bytes 487585 | tf_op jit(solution)/shard_map/while/body/eval_jaxpr/jit(_where)/select_n | solution.py:105
  174.6 4.6 %multiply_select_fusion.19 = f32[16,2,256]{2,0,1:T(8,128)S(1)} fusion(f32[16,2,256]{2,0,1:T(8,128)S(1)} %get-tuple-element.1480, pred[16]{0:T(512)(128)(4,1)S(1)} %get-tuple-element.1435, pred[16]{0:T(512)(128)(4,1)S(1)} %get-tuple-element.1436, pred[16]{0:T(512)(128)(4,1)S(1)} %get-tuple-element.1437, pred[16]{0:T(512)(128)(4,1)S(1)} %get-tuple-element.1438, ...), kind=kLoop, calls=%fused_computation.12.clone.1 | loop fusion | flops 8577024 | bytes 454785 | tf_op jit(solution)/shard_map/while/body/eval_jaxpr/jit(_where)/select_n | solution.py:106
  179.2 2.4 constant_dynamic-slice_fusion.17
  186.3 5.0 %multiply_select_fusion.18 = (f32[16,2,256]{2,0,1:T(8,128)S(1)}, f32[16,2,256]{2,0,1:T(8,128)S(1)}) fusion(f32[16,2,256]{2,0,1:T(8,128)S(1)} %get-tuple-element.1479, pred[16]{0:T(512)(128)(4,1)S(1)} %get-tuple-element.1137, pred[16]{0:T(512)(128)(4,1)S(1)} %get-tuple-element.1138, pred[16]{0:T(512)(128)(4,1)S(1)} %get-tuple-element.1139, ...), kind=kLoop, calls=%fused_computation.20.clone.1 | loop fusion | flops 9216000 | bytes 473217 | tf_op jit(solution)/shard_map/while/body/eval_jaxpr/jit(_where)/select_n | solution.py:94
  191.4 4.6 %add_select_fusion.11 = f32[16,2,256]{2,0,1:T(8,128)S(1)} fusion(f32[16,2,256]{2,0,1:T(8,128)S(1)} %get-tuple-element.1481, f32[16,2,256]{2,0,1:T(8,128)S(1)} %get-tuple-element.1480, f32[]{:T(128)S(6)} %add.8789, f32[]{:T(128)S(6)} %add.8790, f32[]{:T(128)S(6)} %add.8791, f32[]{:T(128)S(6)} %add.8792, f32[]{:T(128)S(6)} %add.8793, f32[]{:T(128)S(6)} %add.8794, ...), kind=kLoop, calls=%fused_computation.4.clone.1 | loop fusion | flops 8822784 | bytes 487585 | tf_op jit(solution)/shard_map/while/body/eval_jaxpr/jit(_where)/select_n | solution.py:105
  196.0 4.6 %multiply_select_fusion.19 = f32[16,2,256]{2,0,1:T(8,128)S(1)} fusion(f32[16,2,256]{2,0,1:T(8,128)S(1)} %get-tuple-element.1480, pred[16]{0:T(512)(128)(4,1)S(1)} %get-tuple-element.1435, pred[16]{0:T(512)(128)(4,1)S(1)} %get-tuple-element.1436, pred[16]{0:T(512)(128)(4,1)S(1)} %get-tuple-element.1437, pred[16]{0:T(512)(128)(4,1)S(1)} %get-tuple-element.1438, ...), kind=kLoop, calls=%fused_computation.12.clone.1 | loop fusion | flops 8577024 | bytes 454785 | tf_op jit(solution)/shard_map/while/body/eval_jaxpr/jit(_where)/select_n | solution.py:106
  200.7 2.4 constant_dynamic-slice_fusion.17
  207.7 5.0 %multiply_select_fusion.18 = (f32[16,2,256]{2,0,1:T(8,128)S(1)}, f32[16,2,256]{2,0,1:T(8,128)S(1)}) fusion(f32[16,2,256]{2,0,1:T(8,128)S(1)} %get-tuple-element.1479, pred[16]{0:T(512)(128)(4,1)S(1)} %get-tuple-element.1137, pred[16]{0:T(512)(128)(4,1)S(1)} %get-tuple-element.1138, pred[16]{0:T(512)(128)(4,1)S(1)} %get-tuple-element.1139, ...), kind=kLoop, calls=%fused_computation.20.clone.1 | loop fusion | flops 9216000 | bytes 473217 | tf_op jit(solution)/shard_map/while/body/eval_jaxpr/jit(_where)/select_n | solution.py:94
  212.8 4.6 %add_select_fusion.11 = f32[16,2,256]{2,0,1:T(8,128)S(1)} fusion(f32[16,2,256]{2,0,1:T(8,128)S(1)} %get-tuple-element.1481, f32[16,2,256]{2,0,1:T(8,128)S(1)} %get-tuple-element.1480, f32[]{:T(128)S(6)} %add.8789, f32[]{:T(128)S(6)} %add.8790, f32[]{:T(128)S(6)} %add.8791, f32[]{:T(128)S(6)} %add.8792, f32[]{:T(128)S(6)} %add.8793, f32[]{:T(128)S(6)} %add.8794, ...), kind=kLoop, calls=%fused_computation.4.clone.1 | loop fusion | flops 8822784 | bytes 487585 | tf_op jit(solution)/shard_map/while/body/eval_jaxpr/jit(_where)/select_n | solution.py:105
  217.4 4.6 %multiply_select_fusion.19 = f32[16,2,256]{2,0,1:T(8,128)S(1)} fusion(f32[16,2,256]{2,0,1:T(8,128)S(1)} %get-tuple-element.1480, pred[16]{0:T(512)(128)(4,1)S(1)} %get-tuple-element.1435, pred[16]{0:T(512)(128)(4,1)S(1)} %get-tuple-element.1436, pred[16]{0:T(512)(128)(4,1)S(1)} %get-tuple-element.1437, pred[16]{0:T(512)(128)(4,1)S(1)} %get-tuple-element.1438, ...), kind=kLoop, calls=%fused_computation.12.clone.1 | loop fusion | flops 8577024 | bytes 454785 | tf_op jit(solution)/shard_map/while/body/eval_jaxpr/jit(_where)/select_n | solution.py:106
  222.1 2.9 constant_dynamic-slice_fusion.17
  229.7 5.0 %multiply_select_fusion.18 = (f32[16,2,256]{2,0,1:T(8,128)S(1)}, f32[16,2,256]{2,0,1:T(8,128)S(1)}) fusion(f32[16,2,256]{2,0,1:T(8,128)S(1)} %get-tuple-element.1479, pred[16]{0:T(512)(128)(4,1)S(1)} %get-tuple-element.1137, pred[16]{0:T(512)(128)(4,1)S(1)} %get-tuple-element.1138, pred[16]{0:T(512)(128)(4,1)S(1)} %get-tuple-element.1139, ...), kind=kLoop, calls=%fused_computation.20.clone.1 | loop fusion | flops 9216000 | bytes 473217 | tf_op jit(solution)/shard_map/while/body/eval_jaxpr/jit(_where)/select_n | solution.py:94
  234.7 4.6 %add_select_fusion.11 = f32[16,2,256]{2,0,1:T(8,128)S(1)} fusion(f32[16,2,256]{2,0,1:T(8,128)S(1)} %get-tuple-element.1481, f32[16,2,256]{2,0,1:T(8,128)S(1)} %get-tuple-element.1480, f32[]{:T(128)S(6)} %add.8789, f32[]{:T(128)S(6)} %add.8790, f32[]{:T(128)S(6)} %add.8791, f32[]{:T(128)S(6)} %add.8792, f32[]{:T(128)S(6)} %add.8793, f32[]{:T(128)S(6)} %add.8794, ...), kind=kLoop, calls=%fused_computation.4.clone.1 | loop fusion | flops 8822784 | bytes 487585 | tf_op jit(solution)/shard_map/while/body/eval_jaxpr/jit(_where)/select_n | solution.py:105
  239.3 4.6 %multiply_select_fusion.19 = f32[16,2,256]{2,0,1:T(8,128)S(1)} fusion(f32[16,2,256]{2,0,1:T(8,128)S(1)} %get-tuple-element.1480, pred[16]{0:T(512)(128)(4,1)S(1)} %get-tuple-element.1435, pred[16]{0:T(512)(128)(4,1)S(1)} %get-tuple-element.1436, pred[16]{0:T(512)(128)(4,1)S(1)} %get-tuple-element.1437, pred[16]{0:T(512)(128)(4,1)S(1)} %get-tuple-element.1438, ...), kind=kLoop, calls=%fused_computation.12.clone.1 | loop fusion | flops 8577024 | bytes 454785 | tf_op jit(solution)/shard_map/while/body/eval_jaxpr/jit(_where)/select_n | solution.py:106
  244.0 2.4 constant_dynamic-slice_fusion.17
  251.2 5.0 %multiply_select_fusion.18 = (f32[16,2,256]{2,0,1:T(8,128)S(1)}, f32[16,2,256]{2,0,1:T(8,128)S(1)}) fusion(f32[16,2,256]{2,0,1:T(8,128)S(1)} %get-tuple-element.1479, pred[16]{0:T(512)(128)(4,1)S(1)} %get-tuple-element.1137, pred[16]{0:T(512)(128)(4,1)S(1)} %get-tuple-element.1138, pred[16]{0:T(512)(128)(4,1)S(1)} %get-tuple-element.1139, ...), kind=kLoop, calls=%fused_computation.20.clone.1 | loop fusion | flops 9216000 | bytes 473217 | tf_op jit(solution)/shard_map/while/body/eval_jaxpr/jit(_where)/select_n | solution.py:94
  256.2 4.6 %add_select_fusion.11 = f32[16,2,256]{2,0,1:T(8,128)S(1)} fusion(f32[16,2,256]{2,0,1:T(8,128)S(1)} %get-tuple-element.1481, f32[16,2,256]{2,0,1:T(8,128)S(1)} %get-tuple-element.1480, f32[]{:T(128)S(6)} %add.8789, f32[]{:T(128)S(6)} %add.8790, f32[]{:T(128)S(6)} %add.8791, f32[]{:T(128)S(6)} %add.8792, f32[]{:T(128)S(6)} %add.8793, f32[]{:T(128)S(6)} %add.8794, ...), kind=kLoop, calls=%fused_computation.4.clone.1 | loop fusion | flops 8822784 | bytes 487585 | tf_op jit(solution)/shard_map/while/body/eval_jaxpr/jit(_where)/select_n | solution.py:105
  260.8 4.6 %multiply_select_fusion.19 = f32[16,2,256]{2,0,1:T(8,128)S(1)} fusion(f32[16,2,256]{2,0,1:T(8,128)S(1)} %get-tuple-element.1480, pred[16]{0:T(512)(128)(4,1)S(1)} %get-tuple-element.1435, pred[16]{0:T(512)(128)(4,1)S(1)} %get-tuple-element.1436, pred[16]{0:T(512)(128)(4,1)S(1)} %get-tuple-element.1437, pred[16]{0:T(512)(128)(4,1)S(1)} %get-tuple-element.1438, ...), kind=kLoop, calls=%fused_computation.12.clone.1 | loop fusion | flops 8577024 | bytes 454785 | tf_op jit(solution)/shard_map/while/body/eval_jaxpr/jit(_where)/select_n | solution.py:106
  266.4 7.2 %all-to-all-start.4 = ((f32[16,1,2]{2,1,0:T(1,128)}), f32[16,1,2]{2,1,0:T(1,128)S(1)}, u32[]{:S(2)}, u32[]{:S(2)}) async-start(f32[16,1,2]{2,1,0:T(1,128)} %broadcast_in_dim.282), calls=%async_computation.4 | async-start | bytes 16384 | tf_op jit(solution)/shard_map/all_to_all | solution.py:30
  273.9 6.8 %all-to-all-done.4 = f32[16,1,2]{2,1,0:T(1,128)S(1)} async-done(((f32[16,1,2]{2,1,0:T(1,128)}), f32[16,1,2]{2,1,0:T(1,128)S(1)}, u32[]{:S(2)}, u32[]{:S(2)}) %all-to-all-start.4) | async-done | bytes 160 | tf_op jit(solution)/shard_map/all_to_all | solution.py:30
  282.8 3.5 %all-to-all-start.5 = ((f32[16,1,4]{2,1,0:T(1,128)}), f32[16,1,4]{2,1,0:T(1,128)S(1)}, u32[]{:S(2)}, u32[]{:S(2)}) async-start(f32[16,1,4]{2,1,0:T(1,128)} %broadcast_in_dim.285), calls=%async_computation.5 | async-start | bytes 16384 | tf_op jit(solution)/shard_map/all_to_all | solution.py:30
  286.9 6.6 %all-to-all-done.5 = f32[16,1,4]{2,1,0:T(1,128)S(1)} async-done(((f32[16,1,4]{2,1,0:T(1,128)}), f32[16,1,4]{2,1,0:T(1,128)S(1)}, u32[]{:S(2)}, u32[]{:S(2)}) %all-to-all-start.5) | async-done | bytes 288 | tf_op jit(solution)/shard_map/all_to_all | solution.py:30
  (398 shorter events, 51.7 us)
Async XLA Ops:
  0.6 33.7 %copy-start = (bf16[200,2,1024]{2,1,0:T(2,128)(2,1)S(1)}, bf16[200,2,1024]{2,1,0:T(2,128)(2,1)}, u32[]{:S(2)}) copy-start(bf16[200,2,1024]{2,1,0:T(2,128)(2,1)} %param.14) | copy-start | bytes 2457604
  2.6 15.4 %all-to-all-start.2 = ((s32[16,1,4]{2,1,0:T(1,128)}), s32[16,1,4]{2,1,0:T(1,128)S(1)}, u32[]{:S(2)}, u32[]{:S(2)}) async-start(s32[16,1,4]{2,1,0:T(1,128)} %copy.1376), calls=%async_computation.2 | async-start | bytes 16384 | tf_op jit(solution)/shard_map/all_to_all | solution.py:171
  18.7 15.7 %all-to-all-start = ((bf16[16,2,200]{2,1,0:T(2,128)(2,1)}), bf16[16,2,200]{2,1,0:T(2,128)(2,1)S(1)}, u32[]{:S(2)}, u32[]{:S(2)}) async-start(bf16[16,2,200]{2,1,0:T(2,128)(2,1)} %broadcast_in_dim.279), calls=%async_computation | async-start | bytes 32768 | tf_op jit(solution)/shard_map/all_to_all | solution.py:30
  35.5 19.2 %copy-start.6 = (s32[16]{0:T(128)S(1)}, s32[16]{0:T(128)}, u32[]{:S(2)}) copy-start(s32[16]{0:T(128)} %param.19) | copy-start | bytes 196
  35.5 19.4 %copy-start.1 = (f32[64,2048]{1,0:T(8,128)S(1)}, f32[64,2048]{1,0:T(8,128)}, u32[]{:S(2)}) copy-start(f32[64,2048]{1,0:T(8,128)} %param.23) | copy-start | bytes 1572868
  35.5 11.1 %all-to-all-start.1 = ((bf16[2,32,1024]{2,0,1:T(2,128)(2,1)}), bf16[2,32,1024]{2,0,1:T(2,128)(2,1)S(1)}, u32[]{:S(2)}, u32[]{:S(2)}) async-start(bf16[2,32,1024]{2,0,1:T(2,128)(2,1)} %copy.1373), calls=%async_computation.1 | async-start | bytes 262144 | tf_op jit(solution)/shard_map/all_to_all | solution.py:152
  48.3 40.9 %all-to-all-start.3 = ((bf16[16,4,2048]{2,1,0:T(4,128)(2,1)}), bf16[16,4,2048]{2,1,0:T(4,128)(2,1)S(1)}, u32[]{:S(2)}, u32[]{:S(2)}) async-start(bf16[16,4,2048]{2,1,0:T(4,128)(2,1)} %reshape.929), calls=%async_computation.3 | async-start | bytes 524288 | tf_op jit(solution)/shard_map/all_to_all | solution.py:173
  90.3 2.5 copy-start.2
  90.3 2.5 copy-start.3
  92.7 173.0 %copy-start.4 = (f32[16]{0:T(128)S(1)}, f32[16]{0:T(128)}, u32[]{:S(2)}) copy-start(f32[16]{0:T(128)} %param.24) | copy-start | bytes 196
  92.8 180.9 %copy-start.5 = (s32[2]{0:T(128)S(1)}, s32[2]{0:T(128)}, u32[]{:S(2)}) copy-start(s32[2]{0:T(128)} %param.17) | copy-start | bytes 28
  92.8 180.9 %copy-start.7 = (f32[5]{0:T(128)S(1)}, f32[5]{0:T(128)}, u32[]{:S(2)}) copy-start(f32[5]{0:T(128)} %constant.436) | copy-start | bytes 64
  266.4 14.2 %all-to-all-start.4 = ((f32[16,1,2]{2,1,0:T(1,128)}), f32[16,1,2]{2,1,0:T(1,128)S(1)}, u32[]{:S(2)}, u32[]{:S(2)}) async-start(f32[16,1,2]{2,1,0:T(1,128)} %broadcast_in_dim.282), calls=%async_computation.4 | async-start | bytes 16384 | tf_op jit(solution)/shard_map/all_to_all | solution.py:30
  282.8 10.8 %all-to-all-start.5 = ((f32[16,1,4]{2,1,0:T(1,128)}), f32[16,1,4]{2,1,0:T(1,128)S(1)}, u32[]{:S(2)}, u32[]{:S(2)}) async-start(f32[16,1,4]{2,1,0:T(1,128)} %broadcast_in_dim.285), calls=%async_computation.5 | async-start | bytes 16384 | tf_op jit(solution)/shard_map/all_to_all | solution.py:30
where the time goes:
time: 301 us; the launch traced here: 299 us
  other arithmetic  139 us (46%)
  local copies, waits for them, and re-layouts  80.7 us (27%)
  starting transfers between devices  37.5 us (12%)
  waiting for transfers between devices  32.6 us (11%)
  loops' own time  6.69 us (2%)
    select_n x8, other arithmetic, advance(): jnp.where(watched, survival * (1.0 - jax.nn.sigmoid((BARRIER_LOG - worst_...  40.1 us
    select_n x8, other arithmetic, advance(): jnp.where(observed, alive_share * (1.0 - call_prob), alive_share)  37.1 us
    select_n x8, other arithmetic, advance(): jnp.where(observed, paid_value + alive_share * call_prob * coupon, paid_v...  36.7 us
    slice x8, local copies, waits for them, and re-layouts, run_block(): coef_b[inner]  20.3 us
    all_to_all x3, waiting for transfers between devices, copy_for_each(): return lax.all_to_all(copies, axis, split_axis=0, concat_axis=0, tiled=True)  20 us
    all_to_all x3, starting transfers between devices, copy_for_each(): return lax.all_to_all(copies, axis, split_axis=0, concat_axis=0, tiled=True)  19 us
    gather x2, local copies, waits for them, and re-layouts, per_device(): draw_other = normal_table[:, (row_index + TROWS // 2) % TROWS]  17.5 us
    gather x2, local copies, waits for them, and re-layouts, per_device(): draw_first = normal_table[:, row_index]  16.5 us
  transfers between devices with their start and end apart: 6, of which 5 were waited for; matrix products, arithmetic and copies ran while one was open for 13% of the time, Pallas kernels for 0%

commit v1 on v0

v1 whole, which is shorter than its diff:
```python
import math

import jax
import jax.numpy as jnp
import numpy as np
from jax import lax
from jax.experimental import pallas as pl
from jax.experimental.pallas import tpu as pltpu
from jax.sharding import PartitionSpec as P

MAT = 64
COEF = 16
TROWS = 2048
PATHS = 256
ES_TAIL = 4


CORRELATION = 0.6
CORR_COMPLEMENT = 0.8
BARRIER_LOG = -0.35
SMOOTHING = 0.03
COUPON_RATE = 0.08


def joined_along(pieces, dim):
    pieces = jnp.moveaxis(pieces, 0, dim)
    lengths = pieces.shape
    return pieces.reshape(*lengths[:dim], lengths[dim] * lengths[dim + 1], *lengths[dim + 2 :])


def copy_for_each(array, axis):
    copies = jnp.broadcast_to(array, (lax.axis_size(axis), *array.shape))
    return lax.all_to_all(copies, axis, split_axis=0, concat_axis=0, tiled=True)


def gather_directly(array, axis, dim):
    return joined_along(copy_for_each(array, axis), dim)


def of_everyone(array, axis):
    return copy_for_each(array, axis).sum(axis=0)


def combined_pairwise(pieces, combine):
    while len(jax.tree.leaves(pieces)[0]) > 1:
        pieces = jax.vmap(combine)(*(pieces[side::2] for side in (0, 1)))
    return pieces[0]


def joined_all(array, axis, combine):
    pieces = copy_for_each(array, axis)
    return combined_pairwise(pieces, combine)


def power_basis():
    half = COEF // 2
    cheb = np.zeros((half, half))
    cheb[0, 0] = 1.0
    cheb[1, 1] = 1.0
    for k in range(2, half):
        cheb[k, 1:] = 2.0 * cheb[k - 1, :-1]
        cheb[k] -= cheb[k - 2]
    odd = np.zeros((half, half))
    odd[0, 0] = 1.0
    for k in range(1, half):
        odd[k] = 2.0 * cheb[k] - odd[k - 1]
    scale = 2.0 ** np.arange(half)
    conv = np.zeros((COEF, COEF))
    for k in range(half):
        conv[:half, 2 * k] = 0.5 * cheb[k] * scale
        conv[half:, 2 * k + 1] = 0.5 * odd[k] * scale
    return conv


def basis_block():
    return np.kron(np.eye(128 // COEF), power_basis())


def draws_kernel(offsets_ref, table_ref, out_ref, first_ref, second_ref, windows_ref):
    trades = offsets_ref.shape[0]
    root_step = math.sqrt(1.0 / MAT)
    table = table_ref[...]
    far = jnp.concatenate([table[:, TROWS // 2 :], table[:, : TROWS // 2]], axis=1)
    first = root_step * table
    second = root_step * (CORRELATION * table + CORR_COMPLEMENT * far)
    first_ref[:, :TROWS] = first
    first_ref[:, TROWS:] = first[:, :256]
    second_ref[:, :TROWS] = second
    second_ref[:, TROWS:] = second[:, :256]
    low = lax.broadcasted_iota(jnp.int32, (MAT, 128), 1) < 64

    def one_trade(trade, carry):
        offset = offsets_ref[trade]
        base = pl.multiple_of((offset // 128) * 128, 128)
        shift = offset % 128
        near = first_ref[:, pl.ds(base, 384)]
        other = second_ref[:, pl.ds(base, 384)]
        near_at = pltpu.roll(near, 384 - shift, 1)
        near_up = pltpu.roll(near, 320 - shift, 1)
        other_at = pltpu.roll(other, 384 - shift, 1)
        other_down = pltpu.roll(other, (448 - shift) % 384, 1)
        for half in range(2):
            cut = slice(half * 128, half * 128 + 128)
            even = jnp.where(low, near_at[:, cut], other_down[:, cut])
            odd = jnp.where(low, near_up[:, cut], other_at[:, cut])
            row = pl.multiple_of((2 * half * trades + trade) * MAT, MAT)
            windows_ref[pl.ds(row, MAT), :] = even
            row = pl.multiple_of(((2 * half + 1) * trades + trade) * MAT, MAT)
            windows_ref[pl.ds(row, MAT), :] = odd
        return carry

    lax.fori_loop(0, trades, one_trade, 0)

    def one_step(step, carry):
        rows = windows_ref[pl.ds(step, 4 * trades, stride=MAT), :]
        pieces = []
        for group in range(4):
            part = rows[group * trades : (group + 1) * trades]
            pieces += [part, part]
        out_ref[step] = jnp.concatenate(pieces, axis=0).T
        return carry

    lax.fori_loop(0, MAT, one_step, 0)


def path_draws(offsets, normal_table):
    trades = offsets.shape[0]
    return pl.pallas_call(
        draws_kernel,
        out_shape=jax.ShapeDtypeStruct((MAT, 128, 128), jnp.float32),
        in_specs=[
            pl.BlockSpec(memory_space=pltpu.SMEM),
            pl.BlockSpec(memory_space=pltpu.VMEM),
        ],
        out_specs=pl.BlockSpec(memory_space=pltpu.VMEM),
        scratch_shapes=[
            pltpu.VMEM((MAT, TROWS + 256), jnp.float32),
            pltpu.VMEM((MAT, TROWS + 256), jnp.float32),
            pltpu.VMEM((4 * trades * MAT, 128), jnp.float32),
        ],
        name="path_draws",
    )(offsets, normal_table)


BLOCK = 16
TILES = 4


def spread(ref, row):
    return ref[pl.ds(row, 8, stride=0), :]


def paths_kernel(rows_ref, pick_ref, basis_ref, terms_ref, draws_ref, out_ref, coef_ref, state_ref):
    block = pl.program_id(0)

    @pl.when(block == 0)
    def _():
        width = rows_ref.shape[1] // 2
        rows = jnp.concatenate([rows_ref[:, :width], rows_ref[:, width:]], axis=0)
        lane = lax.broadcasted_iota(jnp.int32, (128, 128), 1)
        for leg in range(2):
            pick = jnp.where(lane == pick_ref[:, leg : leg + 1], 1.0, 0.0).astype(jnp.bfloat16)
            chosen = jnp.dot(pick, rows, preferred_element_type=jnp.float32).astype(jnp.bfloat16)
            for part in range(width // 128):
                at = leg * width + part * 128
                coef_ref[at : at + 128, :] = lax.dot_general(
                    basis_ref[...],
                    chosen[:, part * 128 : part * 128 + 128],
                    (((1,), (1,)), ((), ())),
                    preferred_element_type=jnp.float32,
                )
        zeros = jnp.zeros((64, 128), jnp.float32)
        state_ref[0] = zeros
        state_ref[1] = zeros
        state_ref[2] = zeros + 1.0
        state_ref[3] = zeros + 1.0
        state_ref[4] = zeros

    step_size = 1.0 / MAT
    half_count = COEF // 2
    knock_start = spread(terms_ref, 0)
    call_start = spread(terms_ref, 1)
    slope = 0.5 / SMOOTHING
    barrier_shift = -BARRIER_LOG * slope

    def leg_step(logs, leg, step, draw_row):
        row = leg * (MAT * COEF) + step * COEF
        bent = [jnp.tanh(x) for x in logs]
        power = [y * y - 0.5 for y in bent]

        def series(first):
            top = spread(coef_ref, row + first + half_count - 1)
            total = [top] * len(logs)
            for k in range(half_count - 2, -1, -1):
                term = spread(coef_ref, row + first + k)
                total = [s * v + term for s, v in zip(total, power)]
            return total

        even = series(0)
        odd = series(half_count)
        out = []
        for at, x in enumerate(logs):
            vol = 0.275 + 0.225 * jnp.tanh(even[at] + bent[at] * odd[at])
            draw = draws_ref[step % BLOCK, pl.ds(draw_row + at * 8, 8), :]
            out.append(x + vol * (draw - (0.5 * step_size) * vol))
        return out

    for sweep in range(8 // TILES):
        top_row = sweep * TILES * 8

        def load(at):
            return [state_ref[at, top_row + i * 8 : top_row + i * 8 + 8, :] for i in range(TILES)]

        def one_step(step, state):
            first, second, survival, alive, paid = state
            first = leg_step(first, 0, step, top_row)
            second = leg_step(second, 1, step, 64 + top_row)
            worst = [jnp.minimum(a, b) for a, b in zip(first, second)]
            scaled = [w * slope for w in worst]
            watch = jnp.where(step >= knock_start, barrier_shift, 1e6)
            gap = step - call_start
            seen = (gap >= 0) & ((gap & (MAT // 8 - 1)) == 0) & (step < MAT - 1)
            call = jnp.where(seen, 0.0, -1e6)
            coupon = 1.0 + COUPON_RATE * (step + 1).astype(jnp.float32) / MAT
            survival = [
                v * (0.5 + 0.5 * jnp.tanh(w + watch)) for v, w in zip(survival, scaled)
            ]
            called = [a * (0.5 + 0.5 * jnp.tanh(w + call)) for a, w in zip(alive, scaled)]
            paid = [p + c * coupon for p, c in zip(paid, called)]
            alive = [a - c for a, c in zip(alive, called)]
            return (first, second, survival, alive, paid)

        def some_steps(at, state):
            for inner in range(UNROLL):
                state = one_step(block * BLOCK + at * UNROLL + inner, state)
            return state

        state = tuple(load(at) for at in range(5))
        state = lax.fori_loop(0, BLOCK // UNROLL, some_steps, state)
        for at in range(5):
            for i in range(TILES):
                state_ref[at, top_row + i * 8 : top_row + i * 8 + 8, :] = state[at][i]

    @pl.when(block == MAT // BLOCK - 1)
    def _():
        worst = jnp.minimum(state_ref[0], state_ref[1])
        knocked = 1.0 - state_ref[2]
        growth = jnp.exp(worst)
        note = state_ref[4] + state_ref[3] * (1.0 + knocked * jnp.minimum(growth - 1.0, 0.0))
        put = knocked * jnp.maximum(1.0 - growth, 0.0)
        payoff = jnp.where(terms_ref[2:3, :] == 0, note, put)
        total = jnp.sum(payoff, axis=0, keepdims=True)
        total = jnp.broadcast_to(total, (8, 128))
        total = total + pltpu.roll(total, 64, 1)
        total = total + pltpu.roll(total, 32, 1)
        out_ref[...] = total * (1.0 / PATHS)


UNROLL = 4


def path_values(rows, pick, terms, draws):
    whole = lambda *dims: pl.BlockSpec(dims, lambda b: (0,) * len(dims))
    return pl.pallas_call(
        paths_kernel,
        grid=(MAT // BLOCK,),
        out_shape=jax.ShapeDtypeStruct((8, 128), jnp.float32),
        in_specs=[
            whole(*rows.shape),
            whole(*pick.shape),
            whole(128, 128),
            whole(*terms.shape),
            pl.BlockSpec((BLOCK, 128, 128), lambda b: (b, 0, 0)),
        ],
        out_specs=whole(8, 128),
        scratch_shapes=[
            pltpu.VMEM((2 * MAT * COEF + 8, 128), jnp.float32),
            pltpu.VMEM((5, 64, 128), jnp.float32),
        ],
        name="path_values",
    )(rows, pick, jnp.asarray(basis_block(), jnp.bfloat16), terms, draws)


def horizon_scale(class_ids):
    table = jnp.sqrt(jnp.array([1.0, 2.0, 4.0, 6.0, 12.0], jnp.float32))
    hits = class_ids[:, None] == jnp.arange(5, dtype=jnp.int32)[None, :]
    return jnp.sum(jnp.where(hits, table[None, :], 0.0), axis=1)


def keep_worst(first_set, second_set):
    return lax.top_k(jnp.concatenate([first_set, second_set]), first_set.shape[0])[0]


def per_device(
    loadings,
    base_coef,
    shocks,
    scen_class,
    names,
    trade_kind,
    call_start,
    knock_start,
    offsets,
    normal_table,
    book_value,
):
    factors = shocks.shape[1]
    scen_here = shocks.shape[0]
    trades_here = names.shape[0]
    bucket = jnp.arange(factors, dtype=jnp.int32) * 5 // factors
    masked = jnp.where(bucket[None, :] >= scen_class[:, None], shocks, 0.0).astype(jnp.bfloat16)
    everyone = gather_directly(masked, "scen", 0)
    product = jnp.einsum("sf,fum->usm", everyone, loadings, preferred_element_type=jnp.float32)
    own_coef = (product + base_coef[:, None, :].astype(jnp.float32)).astype(jnp.bfloat16)
    owned = lax.all_to_all(own_coef, "scen", split_axis=1, concat_axis=0, tiled=True)
    owned_rows = owned.shape[0]
    row_width = owned.shape[1] * owned.shape[2]
    coef_rows = owned.reshape(owned_rows, row_width)
    leg_names = names.reshape(-1)
    leg_total = leg_names.shape[0]
    width_trade = lax.axis_size("trade")
    cap_slots = max(2, (4 * trades_here + width_trade - 1) // width_trade)
    owner_row = leg_names // owned_rows
    local_row = leg_names % owned_rows
    leg_ids = jnp.arange(leg_total, dtype=jnp.int32)
    same_owner = (owner_row[None, :] == owner_row[:, None]) & (leg_ids[None, :] < leg_ids[:, None])
    slot_rank = jnp.sum(same_owner.astype(jnp.int32), axis=1)
    owner_match = (
        owner_row[None, None, :] == jnp.arange(width_trade, dtype=jnp.int32)[:, None, None]
    )
    slot_match = slot_rank[None, None, :] == jnp.arange(cap_slots, dtype=jnp.int32)[None, :, None]
    wanted_rows = jnp.sum(jnp.where(owner_match & slot_match, local_row[None, None, :], 0), axis=2)
    fetched = coef_rows[
        lax.all_to_all(wanted_rows, "trade", split_axis=0, concat_axis=0, tiled=True)
    ]
    replies = lax.all_to_all(fetched, "trade", split_axis=0, concat_axis=0, tiled=True)
    draws = path_draws(offsets, normal_table)
    lanes = 128 // trades_here
    slot = (owner_row * cap_slots + slot_rank).reshape(trades_here, 2)
    scen_of = (jnp.arange(128, dtype=jnp.int32) // trades_here) % scen_here
    pick = jnp.tile(slot, (lanes, 1)) + (scen_of * (width_trade * cap_slots))[:, None]
    terms = jnp.tile(jnp.stack([knock_start, call_start, trade_kind]), (1, lanes))
    terms = jnp.concatenate([terms, jnp.zeros((13, 128), jnp.int32)])
    values = path_values(replies.reshape(width_trade * cap_slots, row_width), pick, terms, draws)
    trade_value = values[0, : scen_here * trades_here].reshape(scen_here, trades_here).T
    partial_pnl = jnp.sum(trade_value - book_value[:, None], axis=0)
    total_pnl = of_everyone(partial_pnl, "trade")
    desk_pnl = total_pnl / math.sqrt(trades_here * lax.axis_size("trade"))
    losses = -desk_pnl * horizon_scale(scen_class)
    candidates = jnp.concatenate([losses, jnp.full((ES_TAIL,), -1e30, jnp.float32)])
    local_tail = lax.top_k(candidates, ES_TAIL)[0]
    merged_tail = joined_all(local_tail, "scen", keep_worst)
    shortfall = jnp.mean(merged_tail)
    return (trade_value, desk_pnl, shortfall)


def solution(mesh):
    return jax.shard_map(
        per_device,
        mesh=mesh,
        in_specs=(
            P(None, ("trade", "scen"), None),
            P(("trade", "scen"), None),
            P("scen", None),
            P("scen"),
            P("trade", None),
            P("trade"),
            P("trade"),
            P("trade"),
            P("trade"),
            P(),
            P("trade"),
        ),
        out_specs=(P("trade", "scen"), P("scen"), P()),
        check_vma=False,
    )
```

time: 301 us -> 115 us (0.38)
  other arithmetic: 139 us -> 8.35 us
  local copies, waits for them, and re-layouts: 80.7 us -> 8.59 us
  Pallas kernels: 0 us -> 23.9 us
  blocking collectives: 0 us -> 10.1 us
  loops' own time: 6.69 us -> 0 us
  waiting for transfers between devices: 32.6 us -> 26.1 us
  starting transfers between devices: 37.5 us -> 33.9 us
    select_n x24 -> x0, other arithmetic: 114 us -> none  [the longest x8 40.1 us: advance(): jnp.where(watched, survival * (1.0 - jax.nn.sigmoid((BARRIER_LOG - worst_...]
    gather x5 -> x0, local copies, waits for them, and re-layouts: 35 us -> none  [the longest x2 17.5 us: per_device(): draw_other = normal_table[:, (row_index + TROWS // 2) % TROWS]]
    pallas_call x0 -> x2, Pallas kernels: none -> 23.9 us  [the longest x1 13.2 us: path_draws(): pl.pallas_call(draws_kernel, out_shape=jax.ShapeDtypeStruct((MAT, 128, 12...]
    slice x8 -> x1, local copies, waits for them, and re-layouts: 20.3 us -> 0.7 us  [per_device(): values[0, :scen_here * trades_here].reshape(scen_here, trades_here)]
    while x144 -> x0, local copies, waits for them, and re-layouts: 10.5 us -> none
    all_to_all x0 -> x1, blocking collectives: none -> 10.1 us  [copy_for_each(): return lax.all_to_all(copies, axis, split_axis=0, concat_axis=0, tiled=True)]
    all_to_all x3 -> x2, waiting for transfers between devices: 20 us -> 12.6 us  [copy_for_each(): return lax.all_to_all(copies, axis, split_axis=0, concat_axis=0, tiled=True)]
    add x8 -> x2, other arithmetic: 7.85 us -> 0.71 us  [the longest x1 0.7 us: per_device(): jnp.tile(slot, (lanes, 1)) + (scen_of * (width_trade * cap_slots))[:, None]]
  transfers between devices with their start and end apart: 6 -> 5, of which waited for: 5 -> 4; matrix products, arithmetic and copies ran while one was open for 13% -> 4% of each run, Pallas kernels for 0% -> 12%
where the time goes in v1:
time: 115 us; the launch traced here: 114 us
  starting transfers between devices  33.9 us (29%)
  waiting for transfers between devices  26.1 us (23%)
  Pallas kernels  23.9 us (21%)
  blocking collectives  10.1 us (9%)
  local copies, waits for them, and re-layouts  8.59 us (7%)
  other arithmetic  8.35 us (7%)
  between operations  2.58 us (2%)
    all_to_all x2, starting transfers between devices, copy_for_each(): return lax.all_to_all(copies, axis, split_axis=0, concat_axis=0, tiled=True)  15.6 us
    pallas_call x1, Pallas kernels, path_draws(): pl.pallas_call(draws_kernel, out_shape=jax.ShapeDtypeStruct((MAT, 128, 12...  13.2 us
    all_to_all x2, waiting for transfers between devices, copy_for_each(): return lax.all_to_all(copies, axis, split_axis=0, concat_axis=0, tiled=True)  12.6 us
    pallas_call x1, Pallas kernels, path_values(): pl.pallas_call(paths_kernel, grid=(MAT // BLOCK,), out_shape=jax.ShapeDty...  10.7 us
    all_to_all x1, blocking collectives, copy_for_each(): return lax.all_to_all(copies, axis, split_axis=0, concat_axis=0, tiled=True)  10.1 us
    all_to_all x1, starting transfers between devices, per_device(): lax.all_to_all(wanted_rows, 'trade', split_axis=0, concat_axis=0, tiled=T...  8.45 us
    all_to_all x1, waiting for transfers between devices, per_device(): lax.all_to_all(own_coef, 'scen', split_axis=1, concat_axis=0, tiled=True)  7.27 us
    all_to_all x1, starting transfers between devices, per_device(): lax.all_to_all(fetched, 'trade', split_axis=0, concat_axis=0, tiled=True)  6.38 us
  transfers between devices with their start and end apart: 5, of which 4 were waited for; matrix products, arithmetic and copies ran while one was open for 4% of the time, Pallas kernels for 12%

profile of v1, /device:TPU:1, one launch (start us, length us, event | category | flops | bytes accessed | tf_op | source)
XLA Modules:
  0.0 113.9 jit_solution(13873974798664029422)
XLA Ops:
  0.6 0.8 copy.65
  1.5 0.1 reshape.281
  1.6 0.2 convert_reduce_fusion
  1.8 0.1 select_reduce_fusion
  1.9 0.7 copy.66
  2.6 8.4 %all-to-all-start.2 = ((s32[16,1,4]{2,1,0:T(1,128)}), s32[16,1,4]{2,1,0:T(1,128)S(1)}, u32[]{:S(2)}, u32[]{:S(2)}) async-start(s32[16,1,4]{2,1,0:T(1,128)} %copy.66), calls=%async_computation.2 | async-start | bytes 16384 | tf_op jit(solution)/shard_map/all_to_all | solution.py:334
  11.1 0.8 fusion.8
  11.8 6.2 %all-to-all-done.2 = s32[16,1,4]{2,1,0:T(1,128)S(1)} async-done(((s32[16,1,4]{2,1,0:T(1,128)}), s32[16,1,4]{2,1,0:T(1,128)S(1)}, u32[]{:S(2)}, u32[]{:S(2)}) %all-to-all-start.2) | async-done | bytes 288 | tf_op jit(solution)/shard_map/all_to_all | solution.py:334
  18.1 0.6 broadcast_in_dim.31
  18.7 8.3 %all-to-all-start = ((bf16[16,2,200]{2,1,0:T(2,128)(2,1)}), bf16[16,2,200]{2,1,0:T(2,128)(2,1)S(1)}, u32[]{:S(2)}, u32[]{:S(2)}) async-start(bf16[16,2,200]{2,1,0:T(2,128)(2,1)} %broadcast_in_dim.31), calls=%async_computation | async-start | bytes 32768 | tf_op jit(solution)/shard_map/all_to_all | solution.py:33
  27.0 0.7 pad_add_fusion
  27.7 0.7 convert_element_type.17
  28.5 5.9 %all-to-all-done = bf16[16,2,200]{2,1,0:T(2,128)(2,1)S(1)} async-done(((bf16[16,2,200]{2,1,0:T(2,128)(2,1)}), bf16[16,2,200]{2,1,0:T(2,128)(2,1)S(1)}, u32[]{:S(2)}, u32[]{:S(2)}) %all-to-all-start) | async-done | bytes 12832 | tf_op jit(solution)/shard_map/all_to_all | solution.py:33
  34.4 0.4 fusion.1
  34.7 0.8 copy.63
  35.5 3.5 %all-to-all-start.1 = ((bf16[2,32,1024]{2,0,1:T(2,128)(2,1)}), bf16[2,32,1024]{2,0,1:T(2,128)(2,1)S(1)}, u32[]{:S(2)}, u32[]{:S(2)}) async-start(bf16[2,32,1024]{2,0,1:T(2,128)(2,1)} %copy.63), calls=%async_computation.1 | async-start | bytes 262144 | tf_op jit(solution)/shard_map/all_to_all | solution.py:315
  39.1 0.1 reshape.285
  39.2 7.3 %all-to-all-done.1 = bf16[2,32,1024]{2,0,1:T(2,128)(2,1)S(1)} async-done(((bf16[2,32,1024]{2,0,1:T(2,128)(2,1)}), bf16[2,32,1024]{2,0,1:T(2,128)(2,1)S(1)}, u32[]{:S(2)}, u32[]{:S(2)}) %all-to-all-start.1) | async-done | bytes 131104 | tf_op jit(solution)/shard_map/all_to_all | solution.py:315
  46.5 0.1 copy.64
  46.6 0.7 gather_fusion
  47.4 0.8 reshape.284
  48.2 6.4 %all-to-all-start.3 = ((bf16[16,4,2048]{2,1,0:T(4,128)(2,1)}), bf16[16,4,2048]{2,1,0:T(4,128)(2,1)S(1)}, u32[]{:S(2)}, u32[]{:S(2)}) async-start(bf16[16,4,2048]{2,1,0:T(4,128)(2,1)} %reshape.284), calls=%async_computation.3 | async-start | bytes 524288 | tf_op jit(solution)/shard_map/all_to_all | solution.py:336
  54.8 0.7 bitcast_add_fusion.pick_ref
  55.5 0.6 concatenate.18.terms_ref
  56.1 13.2 %path_draws.1.draws_ref = f32[64,128,128]{2,1,0:T(8,128)} custom-call(s32[16]{0:T(128)} %offsets_ref.1, f32[64,2048]{1,0:T(8,128)} %table_ref.1), custom_call_target="tpu_custom_call" | custom-call | tf_op jit(solution)/shard_map/path_draws/pallas_call | solution.py:128
  69.2 0.8 reshape.282.rows_ref
  70.0 10.7 %path_values.1 = f32[8,128]{1,0:T(8,128)} custom-call(bf16[64,2048]{1,0:T(8,128)(2,1)} %reshape.282.rows_ref, s32[128,2]{1,0:T(8,128)} %bitcast_add_fusion.pick_ref, bf16[128,128]{1,0:T(8,128)(2,1)} %constant.121.clone.basis_ref, s32[16,128]{1,0:T(8,128)} %concatenate.18.terms_ref, f32[64,128,128]{2,1,0:T(8,128)} %path_draws.1.draws_ref), custom_call_target="tpu_custom_call" | custom-call | tf_op jit(solution)/shard_map/path_values/pallas_call | solution.py:264
  80.7 0.7 slice_reduce_fusion.1
  81.4 0.1 reshape_squeeze.3
  81.5 0.1 subtract_reduce_fusion
  81.6 0.6 broadcast_in_dim.34
  82.2 7.2 %all-to-all-start.4 = ((f32[16,1,2]{2,1,0:T(1,128)}), f32[16,1,2]{2,1,0:T(1,128)S(1)}, u32[]{:S(2)}, u32[]{:S(2)}) async-start(f32[16,1,2]{2,1,0:T(1,128)} %broadcast_in_dim.34), calls=%async_computation.4 | async-start | bytes 16384 | tf_op jit(solution)/shard_map/all_to_all | solution.py:33
  89.5 0.2 fusion.9
  89.7 6.8 %all-to-all-done.4 = f32[16,1,2]{2,1,0:T(1,128)S(1)} async-done(((f32[16,1,2]{2,1,0:T(1,128)}), f32[16,1,2]{2,1,0:T(1,128)S(1)}, u32[]{:S(2)}, u32[]{:S(2)}) %all-to-all-start.4) | async-done | bytes 160 | tf_op jit(solution)/shard_map/all_to_all | solution.py:33
  96.5 0.5 negate_multiply_fusion
  97.0 1.0 top_k.36
  98.0 10.1 %all_to_all.52 = f32[16,1,4]{2,1,0:T(1,128)S(1)} all-to-all(f32[16,1,4]{2,1,0:T(1,128)S(1)} %broadcast_in_dim.63), channel_id=1, replica_groups=mesh['trade'=16,'scen'=16] {'scen'}, dimensions={0} | all-to-all | bytes 512 | tf_op jit(solution)/shard_map/all_to_all | solution.py:33
  108.2 0.1 slice.38
  108.3 0.1 slice.37
  108.4 0.7 top_k.38
  109.0 0.1 slice.40
  109.1 0.1 slice.39
  109.2 0.7 top_k.44
  109.9 0.1 slice.42
  110.0 0.1 slice.41
  110.1 0.7 top_k.46
  110.9 0.7 top_k.47
  111.5 0.6 slice_reduce_fusion
  (42 shorter events, 0.7 us)
Async XLA Ops:
  0.6 33.7 %copy-start = (bf16[200,2,1024]{2,1,0:T(2,128)(2,1)S(1)}, bf16[200,2,1024]{2,1,0:T(2,128)(2,1)}, u32[]{:S(2)}) copy-start(bf16[200,2,1024]{2,1,0:T(2,128)(2,1)} %param.13) | copy-start | bytes 2457604
  2.6 15.4 %all-to-all-start.2 = ((s32[16,1,4]{2,1,0:T(1,128)}), s32[16,1,4]{2,1,0:T(1,128)S(1)}, u32[]{:S(2)}, u32[]{:S(2)}) async-start(s32[16,1,4]{2,1,0:T(1,128)} %copy.66), calls=%async_computation.2 | async-start | bytes 16384 | tf_op jit(solution)/shard_map/all_to_all | solution.py:334
  18.7 15.7 %all-to-all-start = ((bf16[16,2,200]{2,1,0:T(2,128)(2,1)}), bf16[16,2,200]{2,1,0:T(2,128)(2,1)S(1)}, u32[]{:S(2)}, u32[]{:S(2)}) async-start(bf16[16,2,200]{2,1,0:T(2,128)(2,1)} %broadcast_in_dim.31), calls=%async_computation | async-start | bytes 32768 | tf_op jit(solution)/shard_map/all_to_all | solution.py:33
  35.5 11.0 %all-to-all-start.1 = ((bf16[2,32,1024]{2,0,1:T(2,128)(2,1)}), bf16[2,32,1024]{2,0,1:T(2,128)(2,1)S(1)}, u32[]{:S(2)}, u32[]{:S(2)}) async-start(bf16[2,32,1024]{2,0,1:T(2,128)(2,1)} %copy.63), calls=%async_computation.1 | async-start | bytes 262144 | tf_op jit(solution)/shard_map/all_to_all | solution.py:315
  48.2 21.1 %all-to-all-start.3 = ((bf16[16,4,2048]{2,1,0:T(4,128)(2,1)}), bf16[16,4,2048]{2,1,0:T(4,128)(2,1)S(1)}, u32[]{:S(2)}, u32[]{:S(2)}) async-start(bf16[16,4,2048]{2,1,0:T(4,128)(2,1)} %reshape.284), calls=%async_computation.3 | async-start | bytes 524288 | tf_op jit(solution)/shard_map/all_to_all | solution.py:336
  56.0 25.5 %copy-start.3 = (f32[16]{0:T(128)S(1)}, f32[16]{0:T(128)}, u32[]{:S(2)}) copy-start(f32[16]{0:T(128)} %param.23) | copy-start | bytes 196
  56.0 33.4 %copy-start.2 = (s32[2]{0:T(128)S(1)}, s32[2]{0:T(128)}, u32[]{:S(2)}) copy-start(s32[2]{0:T(128)} %param.16) | copy-start | bytes 28
  56.0 33.4 %copy-start.4 = (f32[5]{0:T(128)S(1)}, f32[5]{0:T(128)}, u32[]{:S(2)}) copy-start(f32[5]{0:T(128)} %constant.131) | copy-start | bytes 64
  81.5 31.3 %copy-start.1 = (f32[2,16]{1,0:T(2,128)}, f32[2,16]{1,0:T(2,128)S(1)}, u32[]{:S(2)}) copy-start(f32[2,16]{1,0:T(2,128)S(1)} %reshape_squeeze.3) | copy-start | bytes 388
  82.2 14.2 %all-to-all-start.4 = ((f32[16,1,2]{2,1,0:T(1,128)}), f32[16,1,2]{2,1,0:T(1,128)S(1)}, u32[]{:S(2)}, u32[]{:S(2)}) async-start(f32[16,1,2]{2,1,0:T(1,128)} %broadcast_in_dim.34), calls=%async_computation.4 | async-start | bytes 16384 | tf_op jit(solution)/shard_map/all_to_all | solution.py:33

commit v2 on v1

--- a/solution.py
+++ b/solution.py
@@ -22,34 +22,9 @@
 COUPON_RATE = 0.08
 
 
-def joined_along(pieces, dim):
-    pieces = jnp.moveaxis(pieces, 0, dim)
-    lengths = pieces.shape
-    return pieces.reshape(*lengths[:dim], lengths[dim] * lengths[dim + 1], *lengths[dim + 2 :])
-
-
-def copy_for_each(array, axis):
-    copies = jnp.broadcast_to(array, (lax.axis_size(axis), *array.shape))
-    return lax.all_to_all(copies, axis, split_axis=0, concat_axis=0, tiled=True)
-
-
-def gather_directly(array, axis, dim):
-    return joined_along(copy_for_each(array, axis), dim)
-
-
-def of_everyone(array, axis):
-    return copy_for_each(array, axis).sum(axis=0)
-
-
-def combined_pairwise(pieces, combine):
-    while len(jax.tree.leaves(pieces)[0]) > 1:
-        pieces = jax.vmap(combine)(*(pieces[side::2] for side in (0, 1)))
-    return pieces[0]
-
-
-def joined_all(array, axis, combine):
-    pieces = copy_for_each(array, axis)
-    return combined_pairwise(pieces, combine)
+def spread_to_all(array, axes):
+    copies = jnp.broadcast_to(array, (lax.axis_size(axes), *array.shape))
+    return lax.all_to_all(copies, axes, split_axis=0, concat_axis=0, tiled=True)
 
 
 def power_basis():
@@ -287,10 +262,6 @@
     return jnp.sum(jnp.where(hits, table[None, :], 0.0), axis=1)
 
 
-def keep_worst(first_set, second_set):
-    return lax.top_k(jnp.concatenate([first_set, second_set]), first_set.shape[0])[0]
-
-
 def per_device(
     loadings,
     base_coef,
@@ -307,34 +278,61 @@
     factors = shocks.shape[1]
     scen_here = shocks.shape[0]
     trades_here = names.shape[0]
+    width_trade = lax.axis_size("trade")
+    width_scen = lax.axis_size("scen")
+    trade_at = lax.axis_index("trade")
+    scen_at = lax.axis_index("scen")
+    everywhere = ("trade", "scen")
+    owned_rows = base_coef.shape[0] * width_scen
+    cap_slots = max(2, (4 * trades_here + width_trade - 1) // width_trade)
+
     bucket = jnp.arange(factors, dtype=jnp.int32) * 5 // factors
-    masked = jnp.where(bucket[None, :] >= scen_class[:, None], shocks, 0.0).astype(jnp.bfloat16)
-    everyone = gather_directly(masked, "scen", 0)
+    masked = jnp.where(bucket[None, :] >= scen_class[:, None], shocks, 0.0)
+    slice_len = 16 * (-(-factors // (16 * width_trade)))
+    masked = jnp.pad(masked, ((0, 0), (0, slice_len * width_trade - factors)))
+    shock_part = lax.dynamic_slice_in_dim(masked, trade_at * slice_len, slice_len, axis=1)
+    leg_names = names.reshape(-1)
+    leg_total = leg_names.shape[0]
+    leg_len = leg_total // width_scen
+    leg_part = lax.dynamic_slice_in_dim(leg_names, scen_at * leg_len, leg_len)
+    parts = [
+        shock_part.reshape(-1),
+        (leg_part // owned_rows).astype(jnp.float32),
+        (leg_part % owned_rows).astype(jnp.float32),
+        scen_class.astype(jnp.float32),
+    ]
+    sent = jnp.concatenate(parts).astype(jnp.bfloat16)
+    heard = spread_to_all(sent[None, :], everywhere)
+    heard = heard.reshape(width_trade, width_scen, sent.shape[0])
+    shock_len = scen_here * slice_len
+    everyone = heard[:, :, :shock_len].reshape(width_trade, width_scen, scen_here, slice_len)
+    everyone = everyone.transpose(1, 2, 0, 3).reshape(width_scen * scen_here, -1)[:, :factors]
+    owner_all = heard[:, :, shock_len : shock_len + leg_len].reshape(width_trade, leg_total)
+    local_all = heard[:, :, shock_len + leg_len : shock_len + 2 * leg_len]
+    local_all = local_all.reshape(width_trade, leg_total).astype(jnp.int32)
+    class_all = heard[0, :, shock_len + 2 * leg_len :].astype(jnp.int32).reshape(-1)
+
     product = jnp.einsum("sf,fum->usm", everyone, loadings, preferred_element_type=jnp.float32)
     own_coef = (product + base_coef[:, None, :].astype(jnp.float32)).astype(jnp.bfloat16)
+    draws = path_draws(offsets, normal_table)
+    own_coef, draws = lax.optimization_barrier((own_coef, draws))
     owned = lax.all_to_all(own_coef, "scen", split_axis=1, concat_axis=0, tiled=True)
-    owned_rows = owned.shape[0]
     row_width = owned.shape[1] * owned.shape[2]
     coef_rows = owned.reshape(owned_rows, row_width)
-    leg_names = names.reshape(-1)
-    leg_total = leg_names.shape[0]
-    width_trade = lax.axis_size("trade")
-    cap_slots = max(2, (4 * trades_here + width_trade - 1) // width_trade)
+
+    leg_ids = jnp.arange(leg_total, dtype=jnp.int32)
+    earlier = leg_ids[None, :] < leg_ids[:, None]
+    mine = owner_all.astype(jnp.int32) == trade_at
+    rank_here = jnp.sum((mine[:, None, :] & earlier[None]).astype(jnp.int32), axis=2)
+    slots = jnp.arange(cap_slots, dtype=jnp.int32)
+    hit = mine[:, None, :] & (rank_here[:, None, :] == slots[None, :, None])
+    wanted = jnp.sum(jnp.where(hit, local_all[:, None, :], 0), axis=2)
+    fetched = coef_rows[wanted]
+    replies = lax.all_to_all(fetched, "trade", split_axis=0, concat_axis=0, tiled=True)
+
     owner_row = leg_names // owned_rows
-    local_row = leg_names % owned_rows
-    leg_ids = jnp.arange(leg_total, dtype=jnp.int32)
-    same_owner = (owner_row[None, :] == owner_row[:, None]) & (leg_ids[None, :] < leg_ids[:, None])
+    same_owner = (owner_row[None, :] == owner_row[:, None]) & earlier
     slot_rank = jnp.sum(same_owner.astype(jnp.int32), axis=1)
-    owner_match = (
-        owner_row[None, None, :] == jnp.arange(width_trade, dtype=jnp.int32)[:, None, None]
-    )
-    slot_match = slot_rank[None, None, :] == jnp.arange(cap_slots, dtype=jnp.int32)[None, :, None]
-    wanted_rows = jnp.sum(jnp.where(owner_match & slot_match, local_row[None, None, :], 0), axis=2)
-    fetched = coef_rows[
-        lax.all_to_all(wanted_rows, "trade", split_axis=0, concat_axis=0, tiled=True)
-    ]
-    replies = lax.all_to_all(fetched, "trade", split_axis=0, concat_axis=0, tiled=True)
-    draws = path_draws(offsets, normal_table)
     lanes = 128 // trades_here
     slot = (owner_row * cap_slots + slot_rank).reshape(trades_here, 2)
     scen_of = (jnp.arange(128, dtype=jnp.int32) // trades_here) % scen_here
@@ -343,14 +341,14 @@
     terms = jnp.concatenate([terms, jnp.zeros((13, 128), jnp.int32)])
     values = path_values(replies.reshape(width_trade * cap_slots, row_width), pick, terms, draws)
     trade_value = values[0, : scen_here * trades_here].reshape(scen_here, trades_here).T
+
     partial_pnl = jnp.sum(trade_value - book_value[:, None], axis=0)
-    total_pnl = of_everyone(partial_pnl, "trade")
-    desk_pnl = total_pnl / math.sqrt(trades_here * lax.axis_size("trade"))
-    losses = -desk_pnl * horizon_scale(scen_class)
-    candidates = jnp.concatenate([losses, jnp.full((ES_TAIL,), -1e30, jnp.float32)])
-    local_tail = lax.top_k(candidates, ES_TAIL)[0]
-    merged_tail = joined_all(local_tail, "scen", keep_worst)
-    shortfall = jnp.mean(merged_tail)
+    parts_all = spread_to_all(partial_pnl[None, :], everywhere)
+    parts_all = parts_all.reshape(width_trade, width_scen * scen_here)
+    pnl_all = jnp.sum(parts_all, axis=0) / math.sqrt(trades_here * width_trade)
+    desk_pnl = lax.dynamic_slice_in_dim(pnl_all, scen_at * scen_here, scen_here)
+    losses = -pnl_all * horizon_scale(class_all)
+    shortfall = jnp.mean(lax.top_k(losses, ES_TAIL)[0])
     return (trade_value, desk_pnl, shortfall)
 
 

time: 115 us -> 111 us (0.965)
  blocking collectives: 10.1 us -> 0 us
  starting transfers between devices: 33.9 us -> 38.7 us
  local copies, waits for them, and re-layouts: 8.59 us -> 9.87 us
    all_to_all x1 -> x0, blocking collectives: 10.1 us -> none  [copy_for_each(): return lax.all_to_all(copies, axis, split_axis=0, concat_axis=0, tiled=True)]
    all_to_all x1, waiting for transfers between devices: 0.01 us -> 7.12 us  [per_device(): lax.all_to_all(fetched, 'trade', split_axis=0, concat_axis=0, tiled=True)]
    all_to_all x3 -> x2, waiting for transfers between devices: 18.9 us -> 13.2 us  [spread_to_all(): return lax.all_to_all(copies, axes, split_axis=0, concat_axis=0, tiled=True)]
    all_to_all x1, starting transfers between devices: 3.51 us -> 8.52 us  [per_device(): lax.all_to_all(own_coef, 'scen', split_axis=1, concat_axis=0, tiled=True)]
    all_to_all x3 -> x2, starting transfers between devices: 24 us -> 21.7 us  [spread_to_all(): return lax.all_to_all(copies, axes, split_axis=0, concat_axis=0, tiled=True)]
    all_to_all x1, starting transfers between devices: 6.38 us -> 8.49 us  [per_device(): lax.all_to_all(fetched, 'trade', split_axis=0, concat_axis=0, tiled=True)]
    top_k x5 -> x1, other arithmetic: 3.62 us -> 1.62 us  [per_device(): shortfall = jnp.mean(lax.top_k(losses, ES_TAIL)[0])]
  transfers between devices with their start and end apart: 5 -> 4, of which waited for: 4 -> 3; matrix products, arithmetic and copies ran while one was open for 4% -> 4% of each run, Pallas kernels for 12% -> 12%
where the time goes in v2:
time: 111 us; the launch traced here: 110 us
  starting transfers between devices  38.7 us (35%)
  waiting for transfers between devices  27 us (24%)
  Pallas kernels  23.9 us (22%)
  local copies, waits for them, and re-layouts  9.87 us (9%)
  other arithmetic  7.93 us (7%)
  between operations  2.66 us (2%)
    all_to_all x2, starting transfers between devices, spread_to_all(): return lax.all_to_all(copies, axes, split_axis=0, concat_axis=0, tiled=True)  21.7 us
    all_to_all x2, waiting for transfers between devices, spread_to_all(): return lax.all_to_all(copies, axes, split_axis=0, concat_axis=0, tiled=True)  13.2 us
    pallas_call x1, Pallas kernels, path_draws(): pl.pallas_call(draws_kernel, out_shape=jax.ShapeDtypeStruct((MAT, 128, 12...  13.1 us
    pallas_call x1, Pallas kernels, path_values(): pl.pallas_call(paths_kernel, grid=(MAT // BLOCK,), out_shape=jax.ShapeDty...  10.7 us
    all_to_all x1, starting transfers between devices, per_device(): lax.all_to_all(own_coef, 'scen', split_axis=1, concat_axis=0, tiled=True)  8.52 us
    all_to_all x1, starting transfers between devices, per_device(): lax.all_to_all(fetched, 'trade', split_axis=0, concat_axis=0, tiled=True)  8.49 us
    all_to_all x1, waiting for transfers between devices, per_device(): lax.all_to_all(fetched, 'trade', split_axis=0, concat_axis=0, tiled=True)  7.12 us
    all_to_all x1, waiting for transfers between devices, per_device(): lax.all_to_all(own_coef, 'scen', split_axis=1, concat_axis=0, tiled=True)  6.72 us
  transfers between devices with their start and end apart: 4, of which 3 were waited for; matrix products, arithmetic and copies ran while one was open for 4% of the time, Pallas kernels for 12%

profile of v2, /device:TPU:1, one launch (start us, length us, event | category | flops | bytes accessed | tf_op | source)
XLA Modules:
  0.0 110.4 jit_solution(2643564314350185949)
XLA Ops:
  0.7 0.8 copy.84
  1.5 0.1 reshape.210
  1.6 0.1 convert_convert_fusion.1
  1.7 0.7 fusion.10
  2.3 0.8 compare_select_fusion.1
  3.2 0.1 reshape.209
  3.3 0.7 broadcast_in_dim.29
  4.1 15.7 %all-to-all-start = ((bf16[256,1,38]{2,1,0:T(2,128)(2,1)}), bf16[256,1,38]{2,1,0:T(2,128)(2,1)S(1)}, u32[]{:S(2)}, u32[]{:S(2)}) async-start(bf16[256,1,38]{2,1,0:T(2,128)(2,1)} %broadcast_in_dim.29), calls=%async_computation | async-start | bytes 262144 | tf_op jit(solution)/shard_map/all_to_all | solution.py:27
  19.8 0.2 convert_reduce_fusion.1
  20.0 0.7 pad_add_fusion
  20.7 0.7 convert_element_type.59
  21.4 13.1 %path_draws.1.draws_ref = f32[64,128,128]{2,1,0:T(8,128)} custom-call(s32[16]{0:T(128)} %offsets_ref.1, f32[64,2048]{1,0:T(8,128)} %table_ref.1), custom_call_target="tpu_custom_call" | custom-call | tf_op jit(solution)/shard_map/path_draws/pallas_call | solution.py:103
  34.6 0.1 fusion.13
  34.7 0.2 copy.102
  34.9 0.1 copy.90
  35.1 0.2 copy.103
  35.4 0.1 reshape.212
  35.6 0.2 reshape.213
  35.8 0.4 fusion.1
  36.2 0.8 copy.87
  37.0 8.5 %all-to-all-start.1 = ((bf16[2,32,1024]{2,0,1:T(2,128)(2,1)}), bf16[2,32,1024]{2,0,1:T(2,128)(2,1)S(1)}, u32[]{:S(2)}, u32[]{:S(2)}) async-start(bf16[2,32,1024]{2,0,1:T(2,128)(2,1)} %copy.87), calls=%async_computation.1 | async-start | bytes 262144 | tf_op jit(solution)/shard_map/all_to_all | solution.py:319
  45.5 0.3 convert_reduce_fusion
  45.8 0.1 select_reduce_fusion
  46.1 0.1 reshape.221
  46.2 6.7 %all-to-all-done.1 = bf16[2,32,1024]{2,0,1:T(2,128)(2,1)S(1)} async-done(((bf16[2,32,1024]{2,0,1:T(2,128)(2,1)}), bf16[2,32,1024]{2,0,1:T(2,128)(2,1)S(1)}, u32[]{:S(2)}, u32[]{:S(2)}) %all-to-all-start.1) | async-done | bytes 131104 | tf_op jit(solution)/shard_map/all_to_all | solution.py:319
  52.9 0.1 copy.88
  53.1 0.7 gather_fusion
  53.8 0.8 reshape.220
  54.6 8.5 %all-to-all-start.2 = ((bf16[16,4,2048]{2,1,0:T(4,128)(2,1)}), bf16[16,4,2048]{2,1,0:T(4,128)(2,1)S(1)}, u32[]{:S(2)}, u32[]{:S(2)}) async-start(bf16[16,4,2048]{2,1,0:T(4,128)(2,1)} %reshape.220), calls=%async_computation.2 | async-start | bytes 524288 | tf_op jit(solution)/shard_map/all_to_all | solution.py:331
  63.2 0.6 concatenate.8.terms_ref
  63.8 0.7 bitcast_add_fusion.pick_ref
  64.6 0.1 reshape.218
  64.7 7.1 %all-to-all-done.2 = bf16[16,4,2048]{2,1,0:T(4,128)(2,1)S(1)} async-done(((bf16[16,4,2048]{2,1,0:T(4,128)(2,1)}), bf16[16,4,2048]{2,1,0:T(4,128)(2,1)S(1)}, u32[]{:S(2)}, u32[]{:S(2)}) %all-to-all-start.2) | async-done | bytes 262176 | tf_op jit(solution)/shard_map/all_to_all | solution.py:331
  71.8 0.7 reshape.215.rows_ref
  72.5 10.7 %path_values.1 = f32[8,128]{1,0:T(8,128)} custom-call(bf16[64,2048]{1,0:T(8,128)(2,1)} %reshape.215.rows_ref, s32[128,2]{1,0:T(8,128)} %bitcast_add_fusion.pick_ref, bf16[128,128]{1,0:T(8,128)(2,1)} %constant.111.clone.basis_ref, s32[16,128]{1,0:T(8,128)} %concatenate.8.terms_ref, f32[64,128,128]{2,1,0:T(8,128)} %path_draws.1.draws_ref), custom_call_target="tpu_custom_call" | custom-call | tf_op jit(solution)/shard_map/path_values/pallas_call | solution.py:239
  83.3 0.7 slice_reduce_fusion.1
  84.0 0.1 reshape_squeeze.3
  84.1 0.1 subtract_reduce_fusion
  84.2 0.7 broadcast_in_dim.32
  84.9 6.0 %all-to-all-start.3 = ((f32[256,1,2]{2,1,0:T(1,128)}), f32[256,1,2]{2,1,0:T(1,128)S(1)}, u32[]{:S(2)}, u32[]{:S(2)}) async-start(f32[256,1,2]{2,1,0:T(1,128)} %broadcast_in_dim.32), calls=%async_computation.3 | async-start | bytes 262144 | tf_op jit(solution)/shard_map/all_to_all | solution.py:27
  90.9 0.1 select_reduce_fusion.1
  91.0 13.2 %all-to-all-done.3 = f32[256,1,2]{2,1,0:T(1,128)S(1)} async-done(((f32[256,1,2]{2,1,0:T(1,128)}), f32[256,1,2]{2,1,0:T(1,128)S(1)}, u32[]{:S(2)}, u32[]{:S(2)}) %all-to-all-start.3) | async-done | bytes 2080 | tf_op jit(solution)/shard_map/all_to_all | solution.py:27
  104.2 0.5 broadcast.240
  104.7 1.0 reduce.7
  105.7 0.1 reshape.216
  105.8 1.6 %top_k.9 = (f32[32]{0:T(128)S(1)}, s32[32]{0:T(128)}) sort(f32[32]{0:T(128)S(1)} %get-tuple-element.14, s32[32]{0:T(128)S(1)} %iota.39), dimensions={0}, to_apply=%region_6.7 | sort | flops 160 | bytes 512 | tf_op jit(solution)/shard_map/top_k | solution.py:351
  107.4 0.6 slice_reduce_fusion
  108.0 0.6 dynamic_slice.11
  (35 shorter events, 1.0 us)
Async XLA Ops:
  0.6 35.2 %copy-start = (bf16[200,2,1024]{2,1,0:T(2,128)(2,1)S(1)}, bf16[200,2,1024]{2,1,0:T(2,128)(2,1)}, u32[]{:S(2)}) copy-start(bf16[200,2,1024]{2,1,0:T(2,128)(2,1)} %param.13) | copy-start | bytes 2457604
  4.1 30.5 %all-to-all-start = ((bf16[256,1,38]{2,1,0:T(2,128)(2,1)}), bf16[256,1,38]{2,1,0:T(2,128)(2,1)S(1)}, u32[]{:S(2)}, u32[]{:S(2)}) async-start(bf16[256,1,38]{2,1,0:T(2,128)(2,1)} %broadcast_in_dim.29), calls=%async_computation | async-start | bytes 262144 | tf_op jit(solution)/shard_map/all_to_all | solution.py:27
  37.0 16.0 %all-to-all-start.1 = ((bf16[2,32,1024]{2,0,1:T(2,128)(2,1)}), bf16[2,32,1024]{2,0,1:T(2,128)(2,1)S(1)}, u32[]{:S(2)}, u32[]{:S(2)}) async-start(bf16[2,32,1024]{2,0,1:T(2,128)(2,1)} %copy.87), calls=%async_computation.1 | async-start | bytes 262144 | tf_op jit(solution)/shard_map/all_to_all | solution.py:319
  53.1 31.0 %copy-start.2 = (f32[16]{0:T(128)S(1)}, f32[16]{0:T(128)}, u32[]{:S(2)}) copy-start(f32[16]{0:T(128)} %param.23) | copy-start | bytes 196
  53.1 37.8 %copy-start.3 = (f32[5]{0:T(128)S(1)}, f32[5]{0:T(128)}, u32[]{:S(2)}) copy-start(f32[5]{0:T(128)} %constant.121) | copy-start | bytes 64
  54.6 17.2 %all-to-all-start.2 = ((bf16[16,4,2048]{2,1,0:T(4,128)(2,1)}), bf16[16,4,2048]{2,1,0:T(4,128)(2,1)S(1)}, u32[]{:S(2)}, u32[]{:S(2)}) async-start(bf16[16,4,2048]{2,1,0:T(4,128)(2,1)} %reshape.220), calls=%async_computation.2 | async-start | bytes 524288 | tf_op jit(solution)/shard_map/all_to_all | solution.py:331
  84.1 25.2 %copy-start.1 = (f32[2,16]{1,0:T(2,128)}, f32[2,16]{1,0:T(2,128)S(1)}, u32[]{:S(2)}) copy-start(f32[2,16]{1,0:T(2,128)S(1)} %reshape_squeeze.3) | copy-start | bytes 388
  84.9 19.3 %all-to-all-start.3 = ((f32[256,1,2]{2,1,0:T(1,128)}), f32[256,1,2]{2,1,0:T(1,128)S(1)}, u32[]{:S(2)}, u32[]{:S(2)}) async-start(f32[256,1,2]{2,1,0:T(1,128)} %broadcast_in_dim.32), calls=%async_computation.3 | async-start | bytes 262144 | tf_op jit(solution)/shard_map/all_to_all | solution.py:27

commit v3 on v2

--- a/solution.py
+++ b/solution.py
@@ -20,11 +20,6 @@
 BARRIER_LOG = -0.35
 SMOOTHING = 0.03
 COUPON_RATE = 0.08
-
-
-def spread_to_all(array, axes):
-    copies = jnp.broadcast_to(array, (lax.axis_size(axes), *array.shape))
-    return lax.all_to_all(copies, axes, split_axis=0, concat_axis=0, tiled=True)
 
 
 def power_basis():
@@ -51,7 +46,7 @@
     return np.kron(np.eye(128 // COEF), power_basis())
 
 
-def draws_kernel(offsets_ref, table_ref, out_ref, first_ref, second_ref, windows_ref):
+def windows_kernel(offsets_ref, table_ref, windows_ref, first_ref, second_ref):
     trades = offsets_ref.shape[0]
     root_step = math.sqrt(1.0 / MAT)
     table = table_ref[...]
@@ -86,23 +81,12 @@
 
     lax.fori_loop(0, trades, one_trade, 0)
 
-    def one_step(step, carry):
-        rows = windows_ref[pl.ds(step, 4 * trades, stride=MAT), :]
-        pieces = []
-        for group in range(4):
-            part = rows[group * trades : (group + 1) * trades]
-            pieces += [part, part]
-        out_ref[step] = jnp.concatenate(pieces, axis=0).T
-        return carry
-
-    lax.fori_loop(0, MAT, one_step, 0)
-
-
-def path_draws(offsets, normal_table):
+
+def path_windows(offsets, normal_table):
     trades = offsets.shape[0]
     return pl.pallas_call(
-        draws_kernel,
-        out_shape=jax.ShapeDtypeStruct((MAT, 128, 128), jnp.float32),
+        windows_kernel,
+        out_shape=jax.ShapeDtypeStruct((4 * trades * MAT, 128), jnp.float32),
         in_specs=[
             pl.BlockSpec(memory_space=pltpu.SMEM),
             pl.BlockSpec(memory_space=pltpu.VMEM),
@@ -111,10 +95,41 @@
         scratch_shapes=[
             pltpu.VMEM((MAT, TROWS + 256), jnp.float32),
             pltpu.VMEM((MAT, TROWS + 256), jnp.float32),
-            pltpu.VMEM((4 * trades * MAT, 128), jnp.float32),
         ],
+        name="path_windows",
+    )(offsets, normal_table)
+
+
+TURN = 8
+
+
+def turn_kernel(first_step, windows_ref, *refs):
+    out_ref = refs[-1]
+    groups = windows_ref.shape[0] // MAT
+    trades = groups // 4
+    start = first_step + pl.program_id(0) * TURN
+    for inner in range(TURN):
+        rows = windows_ref[pl.ds(start + inner, groups, stride=MAT), :]
+        pieces = []
+        for group in range(4):
+            part = rows[group * trades : (group + 1) * trades]
+            pieces += [part, part]
+        out_ref[inner] = jnp.concatenate(pieces, axis=0).T
+
+
+def path_draws(windows, half, earlier=None):
+    blocks = MAT // 2 // TURN
+    operands = [windows] if earlier is None else [windows, earlier]
+    in_specs = [pl.BlockSpec(windows.shape, lambda b: (0, 0)), pl.BlockSpec(memory_space=pl.ANY)]
+    return pl.pallas_call(
+        lambda *refs: turn_kernel(half * (MAT // 2), *refs),
+        grid=(blocks,),
+        out_shape=jax.ShapeDtypeStruct((MAT, 128, 128), jnp.float32),
+        in_specs=in_specs[: len(operands)],
+        out_specs=pl.BlockSpec((TURN, 128, 128), lambda b: (half * blocks + b, 0, 0)),
+        input_output_aliases={} if earlier is None else {1: 0},
         name="path_draws",
-    )(offsets, normal_table)
+    )(*operands)
 
 
 BLOCK = 16
@@ -125,7 +140,10 @@
     return ref[pl.ds(row, 8, stride=0), :]
 
 
-def paths_kernel(rows_ref, pick_ref, basis_ref, terms_ref, draws_ref, out_ref, coef_ref, state_ref):
+def paths_kernel(
+    rows_ref, pick_ref, basis_ref, terms_ref, book_ref, draws_ref,
+    value_ref, sent_ref, coef_ref, state_ref,
+):
     block = pl.program_id(0)
 
     @pl.when(block == 0)
@@ -228,38 +246,164 @@
         total = jnp.broadcast_to(total, (8, 128))
         total = total + pltpu.roll(total, 64, 1)
         total = total + pltpu.roll(total, 32, 1)
-        out_ref[...] = total * (1.0 / PATHS)
+        total = total * (1.0 / PATHS)
+        trades = value_ref.shape[1]
+        value_ref[0:1, :] = total[0:1, :trades]
+        value_ref[1:2, :] = pltpu.roll(total, 128 - trades, 1)[0:1, :trades]
+        gain = total - spread(book_ref, 0)
+        shift = trades // 2
+        while shift:
+            gain = gain + pltpu.roll(gain, shift, 1)
+            shift //= 2
+        lane = lax.broadcasted_iota(jnp.int32, (8, 128), 1)
+        sent = spread(book_ref, 1)
+        sent = jnp.where(lane == 0, pltpu.roll(gain, 129 - trades, 1), sent)
+        sent = jnp.where(lane == 1, pltpu.roll(gain, 130 - 2 * trades, 1), sent)
+        sent_ref[...] = jnp.broadcast_to(sent[0:1, :], sent_ref.shape)
 
 
 UNROLL = 4
 
 
-def path_values(rows, pick, terms, draws):
+def path_values(rows, pick, terms, book, draws, trades, devices):
     whole = lambda *dims: pl.BlockSpec(dims, lambda b: (0,) * len(dims))
     return pl.pallas_call(
         paths_kernel,
         grid=(MAT // BLOCK,),
-        out_shape=jax.ShapeDtypeStruct((8, 128), jnp.float32),
+        out_shape=(
+            jax.ShapeDtypeStruct((2, trades), jnp.float32),
+            jax.ShapeDtypeStruct((devices, 128), jnp.float32),
+        ),
         in_specs=[
             whole(*rows.shape),
             whole(*pick.shape),
             whole(128, 128),
             whole(*terms.shape),
+            whole(*book.shape),
             pl.BlockSpec((BLOCK, 128, 128), lambda b: (b, 0, 0)),
         ],
-        out_specs=whole(8, 128),
+        out_specs=(whole(2, trades), whole(devices, 128)),
         scratch_shapes=[
             pltpu.VMEM((2 * MAT * COEF + 8, 128), jnp.float32),
             pltpu.VMEM((5, 64, 128), jnp.float32),
         ],
         name="path_values",
-    )(rows, pick, jnp.asarray(basis_block(), jnp.bfloat16), terms, draws)
+    )(rows, pick, jnp.asarray(basis_block(), jnp.bfloat16), terms, book, draws)
 
 
 def horizon_scale(class_ids):
     table = jnp.sqrt(jnp.array([1.0, 2.0, 4.0, 6.0, 12.0], jnp.float32))
     hits = class_ids[:, None] == jnp.arange(5, dtype=jnp.int32)[None, :]
     return jnp.sum(jnp.where(hits, table[None, :], 0.0), axis=1)
+
+
+SLICE = 16
+LEG_LANE = 2 * SLICE
+
+
+def pack_kernel(names_ref, class_ref, shocks_ref, out_ref, wide_ref):
+    trade_at = lax.axis_index("trade")
+    scen_at = lax.axis_index("scen")
+    factors = shocks_ref.shape[1]
+    wide = wide_ref.shape[1]
+    wide_ref[...] = jnp.zeros(wide_ref.shape, jnp.float32)
+    wide_ref[0:2, :factors] = shocks_ref[...]
+    row = lax.broadcasted_iota(jnp.int32, wide_ref.shape, 0)
+    lane = lax.broadcasted_iota(jnp.int32, wide_ref.shape, 1)
+    class_of = jnp.where(row == 0, class_ref[0], class_ref[1])
+    masked = jnp.where(lane * 5 >= class_of * factors, wide_ref[...], 0.0)
+    here = pltpu.roll(masked, (wide - trade_at * SLICE) % wide, 1)[:, :128]
+    after = pltpu.roll(here, SLICE, 1)
+    lane = lax.broadcasted_iota(jnp.int32, (1, 128), 1)
+    sent = jnp.where(lane < SLICE, here[0:1, :], after[1:2, :])
+    for leg in range(2):
+        name = names_ref[leg, scen_at].astype(jnp.float32)
+        sent = jnp.where(lane == LEG_LANE + leg, name, sent)
+    out_ref[...] = jnp.broadcast_to(sent, out_ref.shape)
+
+
+def pack(names, scen_class, shocks, devices):
+    return pl.pallas_call(
+        pack_kernel,
+        out_shape=jax.ShapeDtypeStruct((devices, 128), jnp.float32),
+        in_specs=[
+            pl.BlockSpec(memory_space=pltpu.SMEM),
+            pl.BlockSpec(memory_space=pltpu.SMEM),
+            pl.BlockSpec(memory_space=pltpu.VMEM),
+        ],
+        out_specs=pl.BlockSpec(memory_space=pltpu.VMEM),
+        scratch_shapes=[pltpu.VMEM((8, 256), jnp.float32)],
+        name="pack",
+    )(names, scen_class, shocks)
+
+
+def unpack_kernel(heard_ref, out_ref, rows_ref):
+    scens = out_ref.shape[0] // 2
+    lane = lax.broadcasted_iota(jnp.int32, (scens, 128), 1)
+    per_tile = 128 // SLICE
+    for tile in range(2):
+        for scen in range(2):
+            total = jnp.zeros((scens, 128), jnp.float32)
+            for at in range(per_tile):
+                first = (tile * per_tile + at) * scens
+                part = heard_ref[first : first + scens, :]
+                part = pltpu.roll(part, ((at - scen) * SLICE) % 128, 1)
+                total = jnp.where(lane // SLICE == at, part, total)
+            rows_ref[pl.ds(tile * 2 * scens + scen, scens, stride=2), :] = total
+    out_ref[:, :128] = rows_ref[: 2 * scens, :].astype(jnp.bfloat16)
+    out_ref[:, 128:] = rows_ref[2 * scens :, : out_ref.shape[1] - 128].astype(jnp.bfloat16)
+
+
+def unpack(heard, scens, factors):
+    return pl.pallas_call(
+        unpack_kernel,
+        out_shape=jax.ShapeDtypeStruct((2 * scens, factors), jnp.bfloat16),
+        in_specs=[pl.BlockSpec(memory_space=pltpu.VMEM)],
+        out_specs=pl.BlockSpec(memory_space=pltpu.VMEM),
+        scratch_shapes=[pltpu.VMEM((4 * scens, 128), jnp.float32)],
+        name="unpack",
+    )(heard)
+
+
+def tail_kernel(heard_ref, desk_ref, tail_ref):
+    scen_at = lax.axis_index("scen")
+    scens = lax.axis_size("scen")
+    blocks = heard_ref.shape[0] // scens
+    total = heard_ref[0:scens, :]
+    factor = pltpu.roll(total, 64, 1)
+    for block in range(1, blocks):
+        total = total + heard_ref[block * scens : (block + 1) * scens, :]
+    pnl = total / math.sqrt(blocks * 16)
+    row = lax.broadcasted_iota(jnp.int32, (scens, 128), 0)
+    lane = lax.broadcasted_iota(jnp.int32, (scens, 128), 1)
+    order = (row * 128 + lane).astype(jnp.float32)
+    low = -3e38
+    loss = jnp.where(lane < 2, -pnl * factor, low)
+    tail = 0.0
+    for _ in range(ES_TAIL):
+        worst = jnp.max(loss)
+        place = jnp.min(jnp.where(loss == worst, order, 1e9))
+        loss = jnp.where(order == place, low, loss)
+        tail = tail + worst
+    tail_ref[0] = tail * (1.0 / ES_TAIL)
+    for scen in range(2):
+        desk_ref[scen] = jnp.sum(jnp.where((row == scen_at) & (lane == scen), pnl, 0.0))
+
+
+def tail(heard):
+    return pl.pallas_call(
+        tail_kernel,
+        out_shape=(
+            jax.ShapeDtypeStruct((2,), jnp.float32),
+            jax.ShapeDtypeStruct((1,), jnp.float32),
+        ),
+        in_specs=[pl.BlockSpec(memory_space=pltpu.VMEM)],
+        out_specs=(
+            pl.BlockSpec(memory_space=pltpu.SMEM),
+            pl.BlockSpec(memory_space=pltpu.SMEM),
+        ),
+        name="tail",
+    )(heard)
 
 
 def per_device(
@@ -281,56 +425,39 @@
     width_trade = lax.axis_size("trade")
     width_scen = lax.axis_size("scen")
     trade_at = lax.axis_index("trade")
-    scen_at = lax.axis_index("scen")
     everywhere = ("trade", "scen")
+    devices = width_trade * width_scen
     owned_rows = base_coef.shape[0] * width_scen
     cap_slots = max(2, (4 * trades_here + width_trade - 1) // width_trade)
-
-    bucket = jnp.arange(factors, dtype=jnp.int32) * 5 // factors
-    masked = jnp.where(bucket[None, :] >= scen_class[:, None], shocks, 0.0)
-    slice_len = 16 * (-(-factors // (16 * width_trade)))
-    masked = jnp.pad(masked, ((0, 0), (0, slice_len * width_trade - factors)))
-    shock_part = lax.dynamic_slice_in_dim(masked, trade_at * slice_len, slice_len, axis=1)
-    leg_names = names.reshape(-1)
-    leg_total = leg_names.shape[0]
-    leg_len = leg_total // width_scen
-    leg_part = lax.dynamic_slice_in_dim(leg_names, scen_at * leg_len, leg_len)
-    parts = [
-        shock_part.reshape(-1),
-        (leg_part // owned_rows).astype(jnp.float32),
-        (leg_part % owned_rows).astype(jnp.float32),
-        scen_class.astype(jnp.float32),
-    ]
-    sent = jnp.concatenate(parts).astype(jnp.bfloat16)
-    heard = spread_to_all(sent[None, :], everywhere)
-    heard = heard.reshape(width_trade, width_scen, sent.shape[0])
-    shock_len = scen_here * slice_len
-    everyone = heard[:, :, :shock_len].reshape(width_trade, width_scen, scen_here, slice_len)
-    everyone = everyone.transpose(1, 2, 0, 3).reshape(width_scen * scen_here, -1)[:, :factors]
-    owner_all = heard[:, :, shock_len : shock_len + leg_len].reshape(width_trade, leg_total)
-    local_all = heard[:, :, shock_len + leg_len : shock_len + 2 * leg_len]
-    local_all = local_all.reshape(width_trade, leg_total).astype(jnp.int32)
-    class_all = heard[0, :, shock_len + 2 * leg_len :].astype(jnp.int32).reshape(-1)
-
+    leg_total = 2 * trades_here
+
+    sent = pack(names.T, scen_class, shocks, devices)
+    heard = lax.all_to_all(sent, everywhere, split_axis=0, concat_axis=0, tiled=True)
+    everyone = unpack(heard, width_scen, factors)
     product = jnp.einsum("sf,fum->usm", everyone, loadings, preferred_element_type=jnp.float32)
     own_coef = (product + base_coef[:, None, :].astype(jnp.float32)).astype(jnp.bfloat16)
-    draws = path_draws(offsets, normal_table)
-    own_coef, draws = lax.optimization_barrier((own_coef, draws))
+    windows = path_windows(offsets, normal_table)
+    own_coef, windows, heard = lax.optimization_barrier((own_coef, windows, heard))
     owned = lax.all_to_all(own_coef, "scen", split_axis=1, concat_axis=0, tiled=True)
     row_width = owned.shape[1] * owned.shape[2]
     coef_rows = owned.reshape(owned_rows, row_width)
 
+    names_all = heard[:, LEG_LANE : LEG_LANE + 2].astype(jnp.int32).reshape(width_trade, leg_total)
     leg_ids = jnp.arange(leg_total, dtype=jnp.int32)
     earlier = leg_ids[None, :] < leg_ids[:, None]
-    mine = owner_all.astype(jnp.int32) == trade_at
+    mine = names_all // owned_rows == trade_at
+    local_all = names_all % owned_rows
     rank_here = jnp.sum((mine[:, None, :] & earlier[None]).astype(jnp.int32), axis=2)
     slots = jnp.arange(cap_slots, dtype=jnp.int32)
     hit = mine[:, None, :] & (rank_here[:, None, :] == slots[None, :, None])
     wanted = jnp.sum(jnp.where(hit, local_all[:, None, :], 0), axis=2)
     fetched = coef_rows[wanted]
+    draws = path_draws(windows, 0)
+    fetched, draws = lax.optimization_barrier((fetched, draws))
     replies = lax.all_to_all(fetched, "trade", split_axis=0, concat_axis=0, tiled=True)
-
-    owner_row = leg_names // owned_rows
+    draws = path_draws(windows, 1, draws)
+
+    owner_row = names.reshape(-1) // owned_rows
     same_owner = (owner_row[None, :] == owner_row[:, None]) & earlier
     slot_rank = jnp.sum(same_owner.astype(jnp.int32), axis=1)
     lanes = 128 // trades_here
@@ -339,17 +466,14 @@
     pick = jnp.tile(slot, (lanes, 1)) + (scen_of * (width_trade * cap_slots))[:, None]
     terms = jnp.tile(jnp.stack([knock_start, call_start, trade_kind]), (1, lanes))
     terms = jnp.concatenate([terms, jnp.zeros((13, 128), jnp.int32)])
-    values = path_values(replies.reshape(width_trade * cap_slots, row_width), pick, terms, draws)
-    trade_value = values[0, : scen_here * trades_here].reshape(scen_here, trades_here).T
-
-    partial_pnl = jnp.sum(trade_value - book_value[:, None], axis=0)
-    parts_all = spread_to_all(partial_pnl[None, :], everywhere)
-    parts_all = parts_all.reshape(width_trade, width_scen * scen_here)
-    pnl_all = jnp.sum(parts_all, axis=0) / math.sqrt(trades_here * width_trade)
-    desk_pnl = lax.dynamic_slice_in_dim(pnl_all, scen_at * scen_here, scen_here)
-    losses = -pnl_all * horizon_scale(class_all)
-    shortfall = jnp.mean(lax.top_k(losses, ES_TAIL)[0])
-    return (trade_value, desk_pnl, shortfall)
+    factor_row = jnp.pad(horizon_scale(scen_class), (64, 64 - scen_here))
+    book = jnp.stack([jnp.tile(book_value, lanes), factor_row])
+    book = jnp.concatenate([book, jnp.zeros((14, 128), jnp.float32)])
+    rows = replies.reshape(width_trade * cap_slots, row_width)
+    values, parts = path_values(rows, pick, terms, book, draws, trades_here, devices)
+    parts = lax.all_to_all(parts, everywhere, split_axis=0, concat_axis=0, tiled=True)
+    desk_pnl, shortfall = tail(parts)
+    return (values.T, desk_pnl, shortfall[0])
 
 
 def solution(mesh):

time: 111 us -> 103 us (0.928)
  blocking collectives: 0 us -> 21.1 us
  waiting for transfers between devices: 27 us -> 9.56 us
  starting transfers between devices: 38.7 us -> 28.4 us
  Pallas kernels: 23.9 us -> 30 us
  local copies, waits for them, and re-layouts: 9.87 us -> 5.99 us
  other arithmetic: 7.93 us -> 5.38 us
  between operations: 2.66 us -> 0.74 us
    all_to_all x0 -> x1, blocking collectives: none -> 21.1 us  [per_device(): lax.all_to_all(parts, everywhere, split_axis=0, concat_axis=0, tiled=True)]
    all_to_all x2 -> x1, waiting for transfers between devices: 13.2 us -> 4.26 us  [per_device(): lax.all_to_all(sent, everywhere, split_axis=0, concat_axis=0, tiled=True)]
    pallas_call x2 -> x7, Pallas kernels: 23.9 us -> 30 us  [the longest x1 11.2 us: path_values(): pl.pallas_call(paths_kernel, grid=(MAT // BLOCK,), out_shape=(jax.ShapeDt...]
    all_to_all x2 -> x1, starting transfers between devices: 21.7 us -> 15.7 us  [per_device(): lax.all_to_all(sent, everywhere, split_axis=0, concat_axis=0, tiled=True)]
    all_to_all x1, waiting for transfers between devices: 7.12 us -> 2.49 us  [per_device(): lax.all_to_all(fetched, 'trade', split_axis=0, concat_axis=0, tiled=True)]
    all_to_all x1, starting transfers between devices: 8.52 us -> 4.27 us  [per_device(): lax.all_to_all(own_coef, 'scen', split_axis=1, concat_axis=0, tiled=True)]
    all_to_all x1, waiting for transfers between devices: 6.72 us -> 2.81 us  [per_device(): lax.all_to_all(own_coef, 'scen', split_axis=1, concat_axis=0, tiled=True)]
    top_k x1 -> x0, other arithmetic: 1.62 us -> none  [per_device(): shortfall = jnp.mean(lax.top_k(losses, ES_TAIL)[0])]
  transfers between devices with their start and end apart: 4 -> 3, of which waited for: 3 -> 3; matrix products, arithmetic and copies ran while one was open for 4% -> 6% of each run, Pallas kernels for 12% -> 13%
where the time goes in v3:
time: 103 us; the launch traced here: 102 us
  Pallas kernels  30 us (29%)
  starting transfers between devices  28.4 us (28%)
  blocking collectives  21.1 us (20%)
  waiting for transfers between devices  9.56 us (9%)
  local copies, waits for them, and re-layouts  5.99 us (6%)
  other arithmetic  5.38 us (5%)
  matrix products  1.08 us (1%)
    all_to_all x1, blocking collectives, per_device(): lax.all_to_all(parts, everywhere, split_axis=0, concat_axis=0, tiled=True)  21.1 us
    all_to_all x1, starting transfers between devices, per_device(): lax.all_to_all(sent, everywhere, split_axis=0, concat_axis=0, tiled=True)  15.7 us
    pallas_call x1, Pallas kernels, path_values(): pl.pallas_call(paths_kernel, grid=(MAT // BLOCK,), out_shape=(jax.ShapeDt...  11.2 us
    all_to_all x1, starting transfers between devices, per_device(): lax.all_to_all(fetched, 'trade', split_axis=0, concat_axis=0, tiled=True)  8.49 us
    pallas_call x2, Pallas kernels, path_draws(): pl.pallas_call(lambda *refs: turn_kernel(half * (MAT // 2), *refs), grid=...  7.79 us
    pallas_call x1, Pallas kernels, path_windows(): pl.pallas_call(windows_kernel, out_shape=jax.ShapeDtypeStruct((4 * trades...  5.45 us
    all_to_all x1, starting transfers between devices, per_device(): lax.all_to_all(own_coef, 'scen', split_axis=1, concat_axis=0, tiled=True)  4.27 us
    all_to_all x1, waiting for transfers between devices, per_device(): lax.all_to_all(sent, everywhere, split_axis=0, concat_axis=0, tiled=True)  4.26 us
  transfers between devices with their start and end apart: 3, of which 3 were waited for; matrix products, arithmetic and copies ran while one was open for 6% of the time, Pallas kernels for 13%

profile of v3, /device:TPU:1, one launch (start us, length us, event | category | flops | bytes accessed | tf_op | source)
XLA Modules:
  0.0 102.2 jit_solution(7645041728361352028)
XLA Ops:
  0.6 0.0 copy-start
  0.6 1.6 %pack.1 = f32[256,128]{1,0:T(8,128)} custom-call(s32[2,16]{1,0:T(2,128)} %bitcast.40, s32[2]{0:T(128)} %class_ref.1, f32[2,200]{1,0:T(2,128)} %shocks_ref.1), custom_call_target="tpu_custom_call" | custom-call | tf_op jit(solution)/shard_map/pack/pallas_call | solution.py:326
  2.3 15.7 %all-to-all-start = ((f32[256,1,128]{2,1,0:T(1,128)}), f32[256,1,128]{2,1,0:T(1,128)S(1)}, u32[]{:S(2)}, u32[]{:S(2)}) async-start(f32[256,1,128]{2,1,0:T(1,128)} %bitcast.35), calls=%async_computation | async-start | bytes 262144 | tf_op jit(solution)/shard_map/all_to_all | solution.py:435
  18.0 0.8 copy.49
  18.7 0.1 reshape.216
  18.8 0.2 convert_reduce_fusion.1
  19.0 0.9 fusion.12
  19.9 0.7 pad_add_fusion
  20.6 0.7 convert_element_type.21
  21.3 0.1 reduce_sum.44
  21.3 5.5 %path_windows.1.refs_0_ = f32[4096,128]{1,0:T(8,128)} custom-call(s32[16]{0:T(128)} %offsets_ref.1, f32[64,2048]{1,0:T(8,128)} %table_ref.1), custom_call_target="tpu_custom_call" | custom-call | tf_op jit(solution)/shard_map/path_windows/pallas_call | solution.py:87
  26.8 4.3 %all-to-all-done = f32[256,1,128]{2,1,0:T(1,128)S(1)} async-done(((f32[256,1,128]{2,1,0:T(1,128)}), f32[256,1,128]{2,1,0:T(1,128)S(1)}, u32[]{:S(2)}, u32[]{:S(2)}) %all-to-all-start) | async-done | bytes 131104 | tf_op jit(solution)/shard_map/all_to_all | solution.py:435
  31.1 0.0 copy-start.1
  31.1 0.6 copy-done.1
  31.7 1.6 %unpack.1 = bf16[32,200]{1,0:T(8,128)(2,1)} custom-call(f32[256,128]{1,0:T(8,128)} %bitcast.33), custom_call_target="tpu_custom_call" | custom-call | tf_op jit(solution)/shard_map/unpack/pallas_call | solution.py:358
  33.3 0.0 copy-done
  33.3 1.1 %fusion.1 = bf16[2,32,1024]{2,1,0:T(8,128)(2,1)S(1)} fusion(bf16[200,2,1024]{2,1,0:T(2,128)(2,1)S(1)} %copy-done, f32[2,1024]{1,0:T(2,128)S(1)} %convert_element_type.21, bf16[32,200]{1,0:T(8,128)(2,1)} %unpack.1), kind=kOutput, calls=%fused_computation.3 | convolution fusion | flops 26345472 | bytes 971264 | tf_op jit(solution)/shard_map/sf,fum->usm/dot_general | solution.py:437
  34.4 1.0 slice_convert_fusion
  35.4 0.1 reshape.214
  35.6 0.8 copy.46
  36.4 4.3 %all-to-all-start.1 = ((bf16[2,32,1024]{2,0,1:T(2,128)(2,1)}), bf16[2,32,1024]{2,0,1:T(2,128)(2,1)S(1)}, u32[]{:S(2)}, u32[]{:S(2)}) async-start(bf16[2,32,1024]{2,0,1:T(2,128)(2,1)} %copy.46), calls=%async_computation.1 | async-start | bytes 262144 | tf_op jit(solution)/shard_map/all_to_all | solution.py:441
  40.6 0.3 convert_reduce_fusion
  41.0 0.1 select_reduce_fusion
  41.1 0.1 copy.48
  41.2 0.1 reshape.219
  41.3 0.0 copy-start.2
  41.3 3.9 %path_draws.2.refs_1_ = f32[64,128,128]{2,1,0:T(8,128)} custom-call(f32[4096,128]{1,0:T(8,128)} %path_windows.1.refs_0_), custom_call_target="tpu_custom_call" | custom-call | tf_op jit(solution)/shard_map/path_draws/pallas_call | solution.py:124
  45.3 2.8 %all-to-all-done.1 = bf16[2,32,1024]{2,0,1:T(2,128)(2,1)S(1)} async-done(((bf16[2,32,1024]{2,0,1:T(2,128)(2,1)}), bf16[2,32,1024]{2,0,1:T(2,128)(2,1)S(1)}, u32[]{:S(2)}, u32[]{:S(2)}) %all-to-all-start.1) | async-done | bytes 131104 | tf_op jit(solution)/shard_map/all_to_all | solution.py:441
  48.1 0.1 copy.47
  48.2 0.7 gather_fusion
  48.9 0.8 reshape.218
  49.8 8.5 %all-to-all-start.2 = ((bf16[16,4,2048]{2,1,0:T(4,128)(2,1)}), bf16[16,4,2048]{2,1,0:T(4,128)(2,1)S(1)}, u32[]{:S(2)}, u32[]{:S(2)}) async-start(bf16[16,4,2048]{2,1,0:T(4,128)(2,1)} %reshape.218), calls=%async_computation.2 | async-start | bytes 524288 | tf_op jit(solution)/shard_map/all_to_all | solution.py:457
  58.2 0.1 pad_bitcast_fusion
  58.3 0.1 tile.26
  58.4 0.0 copy-done.2
  58.4 0.1 stack_tile.3
  58.5 0.7 bitcast_add_fusion.pick_ref
  59.2 0.6 concatenate.6.terms_ref
  59.8 0.1 pad.8.clone
  59.9 0.7 maximum_maximum_fusion.book_ref
  60.5 3.9 %path_draws.3.draws_ref = f32[64,128,128]{2,1,0:T(8,128)} custom-call(f32[4096,128]{1,0:T(8,128)} %path_windows.1.refs_0_, f32[64,128,128]{2,1,0:T(8,128)} %path_draws.2.refs_1_), custom_call_target="tpu_custom_call", output_to_operand_aliasing={{}: (1, {})} | custom-call | tf_op jit(solution)/shard_map/path_draws/pallas_call | solution.py:124
  64.4 2.5 %all-to-all-done.2 = bf16[16,4,2048]{2,1,0:T(4,128)(2,1)S(1)} async-done(((bf16[16,4,2048]{2,1,0:T(4,128)(2,1)}), bf16[16,4,2048]{2,1,0:T(4,128)(2,1)S(1)}, u32[]{:S(2)}, u32[]{:S(2)}) %all-to-all-start.2) | async-done | bytes 262176 | tf_op jit(solution)/shard_map/all_to_all | solution.py:457
  66.9 0.8 reshape.215.rows_ref
  67.7 11.2 %path_values.1 = (f32[2,16]{1,0:T(2,128)}, f32[256,128]{1,0:T(8,128)}) custom-call(bf16[64,2048]{1,0:T(8,128)(2,1)} %reshape.215.rows_ref, s32[128,2]{1,0:T(8,128)} %bitcast_add_fusion.pick_ref, bf16[128,128]{1,0:T(8,128)(2,1)} %constant.86.clone.basis_ref, s32[16,128]{1,0:T(8,128)} %concatenate.6.terms_ref, f32[16,128]{1,0:T(8,128)} %maximum_maximum_fusion.book_ref, ...), custom_call_target="tpu_custom_call" | custom-call | tf_op jit(solution)/shard_map/path_values/pallas_call | solution.py:270
  78.9 21.1 %all_to_all.42 = f32[256,1,128]{2,1,0:T(1,128)} all-to-all(f32[256,1,128]{2,1,0:T(1,128)} %bitcast.39), channel_id=1, replica_groups=mesh['trade'=16,'scen'=16] {'trade','scen'}, dimensions={0} | all-to-all | bytes 262144 | tf_op jit(solution)/shard_map/all_to_all | solution.py:474
  99.9 2.3 %tail.1 = (f32[2]{0:T(128)}, f32[1]{0:T(128)}) custom-call(f32[256,128]{1,0:T(8,128)} %bitcast.37), custom_call_target="tpu_custom_call" | custom-call | tf_op jit(solution)/shard_map/tail/pallas_call | solution.py:394
  (12 shorter events, 0.1 us)
Async XLA Ops:
  0.6 32.7 %copy-start = (bf16[200,2,1024]{2,1,0:T(2,128)(2,1)S(1)}, bf16[200,2,1024]{2,1,0:T(2,128)(2,1)}, u32[]{:S(2)}) copy-start(bf16[200,2,1024]{2,1,0:T(2,128)(2,1)} %param.13) | copy-start | bytes 2457604
  2.3 28.8 %all-to-all-start = ((f32[256,1,128]{2,1,0:T(1,128)}), f32[256,1,128]{2,1,0:T(1,128)S(1)}, u32[]{:S(2)}, u32[]{:S(2)}) async-start(f32[256,1,128]{2,1,0:T(1,128)} %bitcast.35), calls=%async_computation | async-start | bytes 262144 | tf_op jit(solution)/shard_map/all_to_all | solution.py:435
  31.1 0.6 copy-start.1
  36.4 11.7 %all-to-all-start.1 = ((bf16[2,32,1024]{2,0,1:T(2,128)(2,1)}), bf16[2,32,1024]{2,0,1:T(2,128)(2,1)S(1)}, u32[]{:S(2)}, u32[]{:S(2)}) async-start(bf16[2,32,1024]{2,0,1:T(2,128)(2,1)} %copy.46), calls=%async_computation.1 | async-start | bytes 262144 | tf_op jit(solution)/shard_map/all_to_all | solution.py:441
  41.3 17.1 %copy-start.2 = (f32[16]{0:T(128)S(1)}, f32[16]{0:T(128)}, u32[]{:S(2)}) copy-start(f32[16]{0:T(128)} %param.23) | copy-start | bytes 196
  49.8 17.2 %all-to-all-start.2 = ((bf16[16,4,2048]{2,1,0:T(4,128)(2,1)}), bf16[16,4,2048]{2,1,0:T(4,128)(2,1)S(1)}, u32[]{:S(2)}, u32[]{:S(2)}) async-start(bf16[16,4,2048]{2,1,0:T(4,128)(2,1)} %reshape.218), calls=%async_computation.2 | async-start | bytes 524288 | tf_op jit(solution)/shard_map/all_to_all | solution.py:457

commit v4 on v3

--- a/solution.py
+++ b/solution.py
@@ -1,3 +1,4 @@
+import functools
 import math
 
 import jax
@@ -20,6 +21,10 @@
 BARRIER_LOG = -0.35
 SMOOTHING = 0.03
 COUPON_RATE = 0.08
+
+
+VOL_LOW = 0.05
+VOL_SPAN = 0.225
 
 
 def power_basis():
@@ -46,9 +51,47 @@
     return np.kron(np.eye(128 // COEF), power_basis())
 
 
-def windows_kernel(offsets_ref, table_ref, windows_ref, first_ref, second_ref):
+def label_rows(names_ref, class_ref, knock_ref, call_ref, kind_ref, book_ref, count_ref, owned_rows, cap_slots):
+    trades = knock_ref.shape[0]
+    owners = count_ref.shape[0]
+    lane = lax.broadcasted_iota(jnp.int32, (1, 128), 1)
+    trade_of = lane % trades
+    for owner in range(owners):
+        count_ref[owner] = 0
+    rows = [jnp.zeros((1, 128), jnp.int32)] * 5
+    book = jnp.zeros((1, 128), jnp.float32)
+    for trade in range(trades):
+        here = trade_of == trade
+        scalars = [knock_ref[trade], call_ref[trade], kind_ref[trade]]
+        for leg in range(2):
+            owner = names_ref[leg, trade] // owned_rows
+            rank = count_ref[owner]
+            count_ref[owner] = rank + 1
+            scalars.append(owner * cap_slots + rank)
+        rows = [jnp.where(here, x, row) for x, row in zip(scalars, rows)]
+        book = jnp.where(here, book_ref[trade], book)
+    scen_shift = jnp.where((lane // trades) % 2 == 1, owners * cap_slots, 0)
+    rows = rows[:3] + [row + scen_shift for row in rows[3:]]
+    class_of = jnp.where(lane == 64, class_ref[0], jnp.where(lane == 65, class_ref[1], -1))
+    factor = jnp.zeros((1, 128), jnp.float32)
+    for at, weeks in enumerate((1.0, 2.0, 4.0, 6.0, 12.0)):
+        factor = jnp.where(class_of == at, math.sqrt(weeks), factor)
+    return rows, [book, factor]
+
+
+def windows_kernel(
+    offsets_ref, names_ref, class_ref, knock_ref, call_ref, kind_ref, book_ref, table_ref,
+    windows_ref, terms_ref, amounts_ref, first_ref, second_ref, count_ref, *, owned_rows, cap_slots,
+):
+    rows, amounts = label_rows(
+        names_ref, class_ref, knock_ref, call_ref, kind_ref, book_ref, count_ref, owned_rows, cap_slots
+    )
+    for at, row in enumerate(rows):
+        terms_ref[at : at + 1, :] = row
+    for at, row in enumerate(amounts):
+        amounts_ref[at : at + 1, :] = row
     trades = offsets_ref.shape[0]
-    root_step = math.sqrt(1.0 / MAT)
+    root_step = VOL_SPAN * math.sqrt(1.0 / MAT)
     table = table_ref[...]
     far = jnp.concatenate([table[:, TROWS // 2 :], table[:, : TROWS // 2]], axis=1)
     first = root_step * table
@@ -82,22 +125,26 @@
     lax.fori_loop(0, trades, one_trade, 0)
 
 
-def path_windows(offsets, normal_table):
+def path_windows(offsets, names, scen_class, knock, call, kind, book, table, owners, owned_rows, cap_slots):
     trades = offsets.shape[0]
+    scalars = pl.BlockSpec(memory_space=pltpu.SMEM)
+    vector = pl.BlockSpec(memory_space=pltpu.VMEM)
     return pl.pallas_call(
-        windows_kernel,
-        out_shape=jax.ShapeDtypeStruct((4 * trades * MAT, 128), jnp.float32),
-        in_specs=[
-            pl.BlockSpec(memory_space=pltpu.SMEM),
-            pl.BlockSpec(memory_space=pltpu.VMEM),
-        ],
-        out_specs=pl.BlockSpec(memory_space=pltpu.VMEM),
+        functools.partial(windows_kernel, owned_rows=owned_rows, cap_slots=cap_slots),
+        out_shape=(
+            jax.ShapeDtypeStruct((4 * trades * MAT, 128), jnp.float32),
+            jax.ShapeDtypeStruct((16, 128), jnp.int32),
+            jax.ShapeDtypeStruct((16, 128), jnp.float32),
+        ),
+        in_specs=[scalars] * 7 + [vector],
+        out_specs=(vector, vector, vector),
         scratch_shapes=[
             pltpu.VMEM((MAT, TROWS + 256), jnp.float32),
             pltpu.VMEM((MAT, TROWS + 256), jnp.float32),
+            pltpu.SMEM((owners,), jnp.int32),
         ],
         name="path_windows",
-    )(offsets, normal_table)
+    )(offsets, names, scen_class, knock, call, kind, book, table)
 
 
 TURN = 8
@@ -141,7 +188,7 @@
 
 
 def paths_kernel(
-    rows_ref, pick_ref, basis_ref, terms_ref, book_ref, draws_ref,
+    rows_ref, basis_ref, terms_ref, book_ref, draws_ref,
     value_ref, sent_ref, coef_ref, state_ref,
 ):
     block = pl.program_id(0)
@@ -150,9 +197,10 @@
     def _():
         width = rows_ref.shape[1] // 2
         rows = jnp.concatenate([rows_ref[:, :width], rows_ref[:, width:]], axis=0)
-        lane = lax.broadcasted_iota(jnp.int32, (128, 128), 1)
+        slot = lax.broadcasted_iota(jnp.int32, (128, 128), 0)
         for leg in range(2):
-            pick = jnp.where(lane == pick_ref[:, leg : leg + 1], 1.0, 0.0).astype(jnp.bfloat16)
+            pick = jnp.where(slot == terms_ref[3 + leg : 4 + leg, :], 1.0, 0.0)
+            pick = pick.T.astype(jnp.bfloat16)
             chosen = jnp.dot(pick, rows, preferred_element_type=jnp.float32).astype(jnp.bfloat16)
             for part in range(width // 128):
                 at = leg * width + part * 128
@@ -193,9 +241,9 @@
         odd = series(half_count)
         out = []
         for at, x in enumerate(logs):
-            vol = 0.275 + 0.225 * jnp.tanh(even[at] + bent[at] * odd[at])
+            vol = VOL_LOW / VOL_SPAN + 1.0 + jnp.tanh(even[at] + bent[at] * odd[at])
             draw = draws_ref[step % BLOCK, pl.ds(draw_row + at * 8, 8), :]
-            out.append(x + vol * (draw - (0.5 * step_size) * vol))
+            out.append(x + vol * (draw - (0.5 * step_size * VOL_SPAN**2) * vol))
         return out
 
     for sweep in range(8 // TILES):
@@ -214,13 +262,13 @@
             gap = step - call_start
             seen = (gap >= 0) & ((gap & (MAT // 8 - 1)) == 0) & (step < MAT - 1)
             call = jnp.where(seen, 0.0, -1e6)
+            passed = step % BLOCK
             coupon = 1.0 + COUPON_RATE * (step + 1).astype(jnp.float32) / MAT
-            survival = [
-                v * (0.5 + 0.5 * jnp.tanh(w + watch)) for v, w in zip(survival, scaled)
-            ]
-            called = [a * (0.5 + 0.5 * jnp.tanh(w + call)) for a, w in zip(alive, scaled)]
-            paid = [p + c * coupon for p, c in zip(paid, called)]
-            alive = [a - c for a, c in zip(alive, called)]
+            coupon = coupon * (1 << (BLOCK - 1 - passed)).astype(jnp.float32) * 2.0**-BLOCK
+            survival = [v + v * jnp.tanh(w + watch) for v, w in zip(survival, scaled)]
+            part = [a * jnp.tanh(w + call) for a, w in zip(alive, scaled)]
+            paid = [p + (a + c) * coupon for p, a, c in zip(paid, alive, part)]
+            alive = [a - c for a, c in zip(alive, part)]
             return (first, second, survival, alive, paid)
 
         def some_steps(at, state):
@@ -232,7 +280,8 @@
         state = lax.fori_loop(0, BLOCK // UNROLL, some_steps, state)
         for at in range(5):
             for i in range(TILES):
-                state_ref[at, top_row + i * 8 : top_row + i * 8 + 8, :] = state[at][i]
+                value = state[at][i] * 2.0**-BLOCK if at in (2, 3) else state[at][i]
+                state_ref[at, top_row + i * 8 : top_row + i * 8 + 8, :] = value
 
     @pl.when(block == MAT // BLOCK - 1)
     def _():
@@ -265,7 +314,7 @@
 UNROLL = 4
 
 
-def path_values(rows, pick, terms, book, draws, trades, devices):
+def path_values(rows, terms, book, draws, trades, devices):
     whole = lambda *dims: pl.BlockSpec(dims, lambda b: (0,) * len(dims))
     return pl.pallas_call(
         paths_kernel,
@@ -276,7 +325,6 @@
         ),
         in_specs=[
             whole(*rows.shape),
-            whole(*pick.shape),
             whole(128, 128),
             whole(*terms.shape),
             whole(*book.shape),
@@ -288,13 +336,7 @@
             pltpu.VMEM((5, 64, 128), jnp.float32),
         ],
         name="path_values",
-    )(rows, pick, jnp.asarray(basis_block(), jnp.bfloat16), terms, book, draws)
-
-
-def horizon_scale(class_ids):
-    table = jnp.sqrt(jnp.array([1.0, 2.0, 4.0, 6.0, 12.0], jnp.float32))
-    hits = class_ids[:, None] == jnp.arange(5, dtype=jnp.int32)[None, :]
-    return jnp.sum(jnp.where(hits, table[None, :], 0.0), axis=1)
+    )(rows, jnp.asarray(basis_block(), jnp.bfloat16), terms, book, draws)
 
 
 SLICE = 16
@@ -376,16 +418,20 @@
     pnl = total / math.sqrt(blocks * 16)
     row = lax.broadcasted_iota(jnp.int32, (scens, 128), 0)
     lane = lax.broadcasted_iota(jnp.int32, (scens, 128), 1)
-    order = (row * 128 + lane).astype(jnp.float32)
-    low = -3e38
-    loss = jnp.where(lane < 2, -pnl * factor, low)
-    tail = 0.0
-    for _ in range(ES_TAIL):
-        worst = jnp.max(loss)
-        place = jnp.min(jnp.where(loss == worst, order, 1e9))
-        loss = jnp.where(order == place, low, loss)
-        tail = tail + worst
-    tail_ref[0] = tail * (1.0 / ES_TAIL)
+    loss = -pnl * factor
+    turned = jnp.concatenate([loss] * (128 // scens), axis=0).T
+    other = lane % scens
+    picked = jnp.zeros((1, 128), jnp.float32)
+    for scen in range(2):
+        mine = turned[scen : scen + 1, :]
+        above = jnp.zeros((scens, 128), jnp.float32)
+        for rival in range(2):
+            theirs = jnp.broadcast_to(loss[:, rival : rival + 1], (scens, 128))
+            first = 2 * row + rival < 2 * other + scen
+            above = above + jnp.where((theirs > mine) | ((theirs == mine) & first), 1.0, 0.0)
+        rank = jnp.sum(above, axis=0, keepdims=True)
+        picked = picked + jnp.where((rank < ES_TAIL) & (lane[0:1] < scens), mine, 0.0)
+    tail_ref[0] = jnp.sum(picked) * (1.0 / ES_TAIL)
     for scen in range(2):
         desk_ref[scen] = jnp.sum(jnp.where((row == scen_at) & (lane == scen), pnl, 0.0))
 
@@ -436,7 +482,10 @@
     everyone = unpack(heard, width_scen, factors)
     product = jnp.einsum("sf,fum->usm", everyone, loadings, preferred_element_type=jnp.float32)
     own_coef = (product + base_coef[:, None, :].astype(jnp.float32)).astype(jnp.bfloat16)
-    windows = path_windows(offsets, normal_table)
+    windows, terms, book = path_windows(
+        offsets, names.T, scen_class, knock_start, call_start, trade_kind, book_value,
+        normal_table, width_trade, owned_rows, cap_slots,
+    )
     own_coef, windows, heard = lax.optimization_barrier((own_coef, windows, heard))
     owned = lax.all_to_all(own_coef, "scen", split_axis=1, concat_axis=0, tiled=True)
     row_width = owned.shape[1] * owned.shape[2]
@@ -457,20 +506,8 @@
     replies = lax.all_to_all(fetched, "trade", split_axis=0, concat_axis=0, tiled=True)
     draws = path_draws(windows, 1, draws)
 
-    owner_row = names.reshape(-1) // owned_rows
-    same_owner = (owner_row[None, :] == owner_row[:, None]) & earlier
-    slot_rank = jnp.sum(same_owner.astype(jnp.int32), axis=1)
-    lanes = 128 // trades_here
-    slot = (owner_row * cap_slots + slot_rank).reshape(trades_here, 2)
-    scen_of = (jnp.arange(128, dtype=jnp.int32) // trades_here) % scen_here
-    pick = jnp.tile(slot, (lanes, 1)) + (scen_of * (width_trade * cap_slots))[:, None]
-    terms = jnp.tile(jnp.stack([knock_start, call_start, trade_kind]), (1, lanes))
-    terms = jnp.concatenate([terms, jnp.zeros((13, 128), jnp.int32)])
-    factor_row = jnp.pad(horizon_scale(scen_class), (64, 64 - scen_here))
-    book = jnp.stack([jnp.tile(book_value, lanes), factor_row])
-    book = jnp.concatenate([book, jnp.zeros((14, 128), jnp.float32)])
     rows = replies.reshape(width_trade * cap_slots, row_width)
-    values, parts = path_values(rows, pick, terms, book, draws, trades_here, devices)
+    values, parts = path_values(rows, terms, book, draws, trades_here, devices)
     parts = lax.all_to_all(parts, everywhere, split_axis=0, concat_axis=0, tiled=True)
     desk_pnl, shortfall = tail(parts)
     return (values.T, desk_pnl, shortfall[0])

time: 103 us -> 98.6 us (0.957)
  waiting for transfers between devices: 9.56 us -> 13.3 us
  other arithmetic: 5.38 us -> 2.24 us
  starting transfers between devices: 28.4 us -> 25.9 us
  local copies, waits for them, and re-layouts: 5.99 us -> 4.16 us
    all_to_all x1, waiting for transfers between devices: 4.26 us -> 6.81 us  [per_device(): lax.all_to_all(sent, everywhere, split_axis=0, concat_axis=0, tiled=True)]
    all_to_all x1, waiting for transfers between devices: 2.49 us -> 4.79 us  [per_device(): lax.all_to_all(fetched, 'trade', split_axis=0, concat_axis=0, tiled=True)]
    all_to_all x1, starting transfers between devices: 8.49 us -> 6.75 us  [per_device(): lax.all_to_all(fetched, 'trade', split_axis=0, concat_axis=0, tiled=True)]
    all_to_all x1, waiting for transfers between devices: 2.81 us -> 1.66 us  [per_device(): lax.all_to_all(own_coef, 'scen', split_axis=1, concat_axis=0, tiled=True)]
    reduce_sum x2 -> x0, other arithmetic: 1.04 us -> none  [the longest x1 0.86 us: horizon_scale(): return jnp.sum(jnp.where(hits, table[None, :], 0.0), axis=1)]
  transfers between devices with their start and end apart: 3 -> 3, of which waited for: 3 -> 3; matrix products, arithmetic and copies ran while one was open for 6% -> 3% of each run, Pallas kernels for 13% -> 14%
where the time goes in v4:
time: 98.6 us; the launch traced here: 98 us
  Pallas kernels  29.8 us (30%)
  starting transfers between devices  25.9 us (26%)
  blocking collectives  20.9 us (21%)
  waiting for transfers between devices  13.3 us (13%)
  local copies, waits for them, and re-layouts  4.16 us (4%)
  other arithmetic  2.24 us (2%)
  matrix products  1.08 us (1%)
    all_to_all x1, blocking collectives, per_device(): lax.all_to_all(parts, everywhere, split_axis=0, concat_axis=0, tiled=True)  20.9 us
    all_to_all x1, starting transfers between devices, per_device(): lax.all_to_all(sent, everywhere, split_axis=0, concat_axis=0, tiled=True)  15.7 us
    pallas_call x1, Pallas kernels, path_values(): pl.pallas_call(paths_kernel, grid=(MAT // BLOCK,), out_shape=(jax.ShapeDt...  11.4 us
    pallas_call x2, Pallas kernels, path_draws(): pl.pallas_call(lambda *refs: turn_kernel(half * (MAT // 2), *refs), grid=...  7.75 us
    all_to_all x1, waiting for transfers between devices, per_device(): lax.all_to_all(sent, everywhere, split_axis=0, concat_axis=0, tiled=True)  6.81 us
    all_to_all x1, starting transfers between devices, per_device(): lax.all_to_all(fetched, 'trade', split_axis=0, concat_axis=0, tiled=True)  6.75 us
    pallas_call x1, Pallas kernels, path_windows(): pl.pallas_call(functools.partial(windows_kernel, owned_rows=owned_rows, c...  5.61 us
    all_to_all x1, waiting for transfers between devices, per_device(): lax.all_to_all(fetched, 'trade', split_axis=0, concat_axis=0, tiled=True)  4.79 us
  transfers between devices with their start and end apart: 3, of which 3 were waited for; matrix products, arithmetic and copies ran while one was open for 3% of the time, Pallas kernels for 14%

profile of v4, /device:TPU:1, one launch (start us, length us, event | category | flops | bytes accessed | tf_op | source)
XLA Modules:
  0.0 98.0 jit_solution(10972995012669825228)
XLA Ops:
  0.6 0.0 copy-start
  0.6 1.6 %pack.1 = f32[256,128]{1,0:T(8,128)} custom-call(s32[2,16]{1,0:T(2,128)} %bitcast.33, s32[2]{0:T(128)} %class_ref.3, f32[2,200]{1,0:T(2,128)} %shocks_ref.1), custom_call_target="tpu_custom_call" | custom-call | tf_op jit(solution)/shard_map/pack/pallas_call | solution.py:368
  2.3 15.7 %all-to-all-start = ((f32[256,1,128]{2,1,0:T(1,128)}), f32[256,1,128]{2,1,0:T(1,128)S(1)}, u32[]{:S(2)}, u32[]{:S(2)}) async-start(f32[256,1,128]{2,1,0:T(1,128)} %bitcast.29), calls=%async_computation | async-start | bytes 262144 | tf_op jit(solution)/shard_map/all_to_all | solution.py:481
  17.9 0.7 convert_element_type.16
  18.6 5.6 %path_windows.1 = (f32[4096,128]{1,0:T(8,128)}, s32[16,128]{1,0:T(8,128)}, f32[16,128]{1,0:T(8,128)}) custom-call(s32[16]{0:T(128)} %offsets_ref.1, s32[2,16]{1,0:T(2,128)} %bitcast.34, s32[2]{0:T(128)} %class_ref.3, s32[16]{0:T(128)} %knock_ref.1, s32[16]{0:T(128)} %call_ref.1, s32[16]{0:T(128)} %kind_ref.1, f32[16]{0:T(128)} %book_ref.1, f32[64,2048]{1,0:T(8,128)} %table_ref.1), custom_call_target="tpu_custom_call" | custom-call | tf_op jit(solution)/shard_map/path_windows/pallas_call | solution.py:132
  24.3 6.8 %all-to-all-done = f32[256,1,128]{2,1,0:T(1,128)S(1)} async-done(((f32[256,1,128]{2,1,0:T(1,128)}), f32[256,1,128]{2,1,0:T(1,128)S(1)}, u32[]{:S(2)}, u32[]{:S(2)}) %all-to-all-start) | async-done | bytes 131104 | tf_op jit(solution)/shard_map/all_to_all | solution.py:481
  31.1 0.0 copy-start.1
  31.1 0.6 copy-done.1
  31.7 1.6 %unpack.1 = bf16[32,200]{1,0:T(8,128)(2,1)} custom-call(f32[256,128]{1,0:T(8,128)} %bitcast.26), custom_call_target="tpu_custom_call" | custom-call | tf_op jit(solution)/shard_map/unpack/pallas_call | solution.py:400
  33.4 0.0 copy-done
  33.4 1.1 %fusion.1 = bf16[2,32,1024]{2,1,0:T(8,128)(2,1)S(1)} fusion(bf16[200,2,1024]{2,1,0:T(2,128)(2,1)S(1)} %copy-done, f32[2,1024]{1,0:T(2,128)S(1)} %convert_element_type.16, bf16[32,200]{1,0:T(8,128)(2,1)} %unpack.1), kind=kOutput, calls=%fused_computation.3 | convolution fusion | flops 26345472 | bytes 971264 | tf_op jit(solution)/shard_map/sf,fum->usm/dot_general | solution.py:483
  34.4 0.8 copy.30
  35.2 3.5 %all-to-all-start.1 = ((bf16[2,32,1024]{2,0,1:T(2,128)(2,1)}), bf16[2,32,1024]{2,0,1:T(2,128)(2,1)S(1)}, u32[]{:S(2)}, u32[]{:S(2)}) async-start(bf16[2,32,1024]{2,0,1:T(2,128)(2,1)} %copy.30), calls=%async_computation.1 | async-start | bytes 262144 | tf_op jit(solution)/shard_map/all_to_all | solution.py:490
  38.8 1.0 %slice_convert_fusion = s32[256,2]{1,0:T(8,128)S(1)} fusion(f32[256,128]{1,0:T(8,128)} %bitcast.27), kind=kLoop, calls=%fused_computation.6 | loop fusion | flops 512 | bytes 4096 | tf_op jit(solution)/shard_map/convert_element_type | solution.py:494
  39.8 0.1 reshape.99
  39.9 0.3 convert_reduce_fusion
  40.3 0.1 select_reduce_fusion
  40.4 0.1 copy.32
  40.5 0.1 reshape.103
  40.6 3.9 %path_draws.2.refs_1_ = f32[64,128,128]{2,1,0:T(8,128)} custom-call(f32[4096,128]{1,0:T(8,128)} %get-tuple-element.18.refs_0_), custom_call_target="tpu_custom_call" | custom-call | tf_op jit(solution)/shard_map/path_draws/pallas_call | solution.py:171
  44.5 1.7 %all-to-all-done.1 = bf16[2,32,1024]{2,0,1:T(2,128)(2,1)S(1)} async-done(((bf16[2,32,1024]{2,0,1:T(2,128)(2,1)}), bf16[2,32,1024]{2,0,1:T(2,128)(2,1)S(1)}, u32[]{:S(2)}, u32[]{:S(2)}) %all-to-all-start.1) | async-done | bytes 131104 | tf_op jit(solution)/shard_map/all_to_all | solution.py:490
  46.1 0.1 copy.31
  46.3 0.7 gather_fusion
  47.0 0.8 reshape.102
  47.8 6.7 %all-to-all-start.2 = ((bf16[16,4,2048]{2,1,0:T(4,128)(2,1)}), bf16[16,4,2048]{2,1,0:T(4,128)(2,1)S(1)}, u32[]{:S(2)}, u32[]{:S(2)}) async-start(bf16[16,4,2048]{2,1,0:T(4,128)(2,1)} %reshape.102), calls=%async_computation.2 | async-start | bytes 524288 | tf_op jit(solution)/shard_map/all_to_all | solution.py:506
  54.6 3.9 %path_draws.3.draws_ref = f32[64,128,128]{2,1,0:T(8,128)} custom-call(f32[4096,128]{1,0:T(8,128)} %get-tuple-element.18.refs_0_, f32[64,128,128]{2,1,0:T(8,128)} %path_draws.2.refs_1_), custom_call_target="tpu_custom_call", output_to_operand_aliasing={{}: (1, {})} | custom-call | tf_op jit(solution)/shard_map/path_draws/pallas_call | solution.py:171
  58.4 4.8 %all-to-all-done.2 = bf16[16,4,2048]{2,1,0:T(4,128)(2,1)S(1)} async-done(((bf16[16,4,2048]{2,1,0:T(4,128)(2,1)}), bf16[16,4,2048]{2,1,0:T(4,128)(2,1)S(1)}, u32[]{:S(2)}, u32[]{:S(2)}) %all-to-all-start.2) | async-done | bytes 262176 | tf_op jit(solution)/shard_map/all_to_all | solution.py:506
  63.2 0.8 reshape.100.rows_ref
  64.0 11.4 %path_values.1 = (f32[2,16]{1,0:T(2,128)}, f32[256,128]{1,0:T(8,128)}) custom-call(bf16[64,2048]{1,0:T(8,128)(2,1)} %reshape.100.rows_ref, bf16[128,128]{1,0:T(8,128)(2,1)} %constant.38.clone.basis_ref, s32[16,128]{1,0:T(8,128)} %get-tuple-element.20.terms_ref, f32[16,128]{1,0:T(8,128)} %get-tuple-element.21.book_ref, f32[64,128,128]{2,1,0:T(8,128)} %path_draws.3.draws_ref), custom_call_target="tpu_custom_call" | custom-call | tf_op jit(solution)/shard_map/path_values/pallas_call | solution.py:319
  75.4 20.9 %all_to_all.42 = f32[256,1,128]{2,1,0:T(1,128)} all-to-all(f32[256,1,128]{2,1,0:T(1,128)} %bitcast.32), channel_id=1, replica_groups=mesh['trade'=16,'scen'=16] {'trade','scen'}, dimensions={0} | all-to-all | bytes 262144 | tf_op jit(solution)/shard_map/all_to_all | solution.py:511
  96.3 1.7 %tail.1 = (f32[2]{0:T(128)}, f32[1]{0:T(128)}) custom-call(f32[256,128]{1,0:T(8,128)} %bitcast.30), custom_call_target="tpu_custom_call" | custom-call | tf_op jit(solution)/shard_map/tail/pallas_call | solution.py:440
  (6 shorter events, 0.1 us)
Async XLA Ops:
  0.6 32.7 %copy-start = (bf16[200,2,1024]{2,1,0:T(2,128)(2,1)S(1)}, bf16[200,2,1024]{2,1,0:T(2,128)(2,1)}, u32[]{:S(2)}) copy-start(bf16[200,2,1024]{2,1,0:T(2,128)(2,1)} %param.12) | copy-start | bytes 2457604
  2.3 28.8 %all-to-all-start = ((f32[256,1,128]{2,1,0:T(1,128)}), f32[256,1,128]{2,1,0:T(1,128)S(1)}, u32[]{:S(2)}, u32[]{:S(2)}) async-start(f32[256,1,128]{2,1,0:T(1,128)} %bitcast.29), calls=%async_computation | async-start | bytes 262144 | tf_op jit(solution)/shard_map/all_to_all | solution.py:481
  31.1 0.6 copy-start.1
  35.2 10.9 %all-to-all-start.1 = ((bf16[2,32,1024]{2,0,1:T(2,128)(2,1)}), bf16[2,32,1024]{2,0,1:T(2,128)(2,1)S(1)}, u32[]{:S(2)}, u32[]{:S(2)}) async-start(bf16[2,32,1024]{2,0,1:T(2,128)(2,1)} %copy.30), calls=%async_computation.1 | async-start | bytes 262144 | tf_op jit(solution)/shard_map/all_to_all | solution.py:490
  47.8 15.4 %all-to-all-start.2 = ((bf16[16,4,2048]{2,1,0:T(4,128)(2,1)}), bf16[16,4,2048]{2,1,0:T(4,128)(2,1)S(1)}, u32[]{:S(2)}, u32[]{:S(2)}) async-start(bf16[16,4,2048]{2,1,0:T(4,128)(2,1)} %reshape.102), calls=%async_computation.2 | async-start | bytes 524288 | tf_op jit(solution)/shard_map/all_to_all | solution.py:506

commit v5 on v4

--- a/solution.py
+++ b/solution.py
@@ -48,7 +48,7 @@
 
 
 def basis_block():
-    return np.kron(np.eye(128 // COEF), power_basis())
+    return np.kron(np.eye(256 // COEF), power_basis())
 
 
 def label_rows(names_ref, class_ref, knock_ref, call_ref, kind_ref, book_ref, count_ref, owned_rows, cap_slots):
@@ -195,21 +195,23 @@
 
     @pl.when(block == 0)
     def _():
-        width = rows_ref.shape[1] // 2
-        rows = jnp.concatenate([rows_ref[:, :width], rows_ref[:, width:]], axis=0)
+        owners, slots, width = rows_ref.shape
+        width //= 2
+        whole_rows = rows_ref[...].reshape(owners * slots, 2 * width)
+        rows = jnp.concatenate([whole_rows[:, :width], whole_rows[:, width:]], axis=0)
         slot = lax.broadcasted_iota(jnp.int32, (128, 128), 0)
-        for leg in range(2):
-            pick = jnp.where(slot == terms_ref[3 + leg : 4 + leg, :], 1.0, 0.0)
-            pick = pick.T.astype(jnp.bfloat16)
-            chosen = jnp.dot(pick, rows, preferred_element_type=jnp.float32).astype(jnp.bfloat16)
-            for part in range(width // 128):
-                at = leg * width + part * 128
-                coef_ref[at : at + 128, :] = lax.dot_general(
-                    basis_ref[...],
-                    chosen[:, part * 128 : part * 128 + 128],
-                    (((1,), (1,)), ((), ())),
-                    preferred_element_type=jnp.float32,
-                )
+        pick = [jnp.where(slot == terms_ref[3 + leg : 4 + leg, :], 1.0, 0.0) for leg in range(2)]
+        pick = jnp.concatenate(pick, axis=1).astype(jnp.bfloat16)
+        chosen = lax.dot_general(
+            rows, pick, (((0,), (0,)), ((), ())), preferred_element_type=jnp.float32
+        ).astype(jnp.bfloat16)
+        part = basis_ref.shape[0]
+        for at in range(0, width, part):
+            terms = jnp.dot(
+                basis_ref[...], chosen[at : at + part], preferred_element_type=jnp.float32
+            )
+            coef_ref[at : at + part, :] = terms[:, :128]
+            coef_ref[width + at : width + at + part, :] = terms[:, 128:]
         zeros = jnp.zeros((64, 128), jnp.float32)
         state_ref[0] = zeros
         state_ref[1] = zeros
@@ -311,7 +313,7 @@
         sent_ref[...] = jnp.broadcast_to(sent[0:1, :], sent_ref.shape)
 
 
-UNROLL = 4
+UNROLL = 8
 
 
 def path_values(rows, terms, book, draws, trades, devices):
@@ -325,7 +327,7 @@
         ),
         in_specs=[
             whole(*rows.shape),
-            whole(128, 128),
+            whole(256, 256),
             whole(*terms.shape),
             whole(*book.shape),
             pl.BlockSpec((BLOCK, 128, 128), lambda b: (b, 0, 0)),
@@ -506,8 +508,7 @@
     replies = lax.all_to_all(fetched, "trade", split_axis=0, concat_axis=0, tiled=True)
     draws = path_draws(windows, 1, draws)
 
-    rows = replies.reshape(width_trade * cap_slots, row_width)
-    values, parts = path_values(rows, terms, book, draws, trades_here, devices)
+    values, parts = path_values(replies, terms, book, draws, trades_here, devices)
     parts = lax.all_to_all(parts, everywhere, split_axis=0, concat_axis=0, tiled=True)
     desk_pnl, shortfall = tail(parts)
     return (values.T, desk_pnl, shortfall[0])

time: 98.6 us -> 98.3 us (level)
  no operation moved by 1% of the time
where the time goes in v5:
time: 98.3 us; the launch traced here: 97.7 us
  Pallas kernels  29.2 us (30%)
  starting transfers between devices  25.9 us (26%)
  blocking collectives  21.1 us (21%)
  waiting for transfers between devices  13.3 us (14%)
  local copies, waits for them, and re-layouts  4.13 us (4%)
  other arithmetic  2.24 us (2%)
  matrix products  1.08 us (1%)
    all_to_all x1, blocking collectives, per_device(): lax.all_to_all(parts, everywhere, split_axis=0, concat_axis=0, tiled=True)  21.1 us
    all_to_all x1, starting transfers between devices, per_device(): lax.all_to_all(sent, everywhere, split_axis=0, concat_axis=0, tiled=True)  15.7 us
    pallas_call x1, Pallas kernels, path_values(): pl.pallas_call(paths_kernel, grid=(MAT // BLOCK,), out_shape=(jax.ShapeDt...  10.8 us
    pallas_call x2, Pallas kernels, path_draws(): pl.pallas_call(lambda *refs: turn_kernel(half * (MAT // 2), *refs), grid=...  7.77 us
    all_to_all x1, waiting for transfers between devices, per_device(): lax.all_to_all(sent, everywhere, split_axis=0, concat_axis=0, tiled=True)  6.83 us
    all_to_all x1, starting transfers between devices, per_device(): lax.all_to_all(fetched, 'trade', split_axis=0, concat_axis=0, tiled=True)  6.73 us
    pallas_call x1, Pallas kernels, path_windows(): pl.pallas_call(functools.partial(windows_kernel, owned_rows=owned_rows, c...  5.6 us
    all_to_all x1, waiting for transfers between devices, per_device(): lax.all_to_all(fetched, 'trade', split_axis=0, concat_axis=0, tiled=True)  4.79 us
  transfers between devices with their start and end apart: 3, of which 3 were waited for; matrix products, arithmetic and copies ran while one was open for 3% of the time, Pallas kernels for 14%

profile of v5, /device:TPU:1, one launch (start us, length us, event | category | flops | bytes accessed | tf_op | source)
XLA Modules:
  0.0 97.7 jit_solution(16726344568663006125)
XLA Ops:
  0.6 0.0 copy-start
  0.6 1.6 %pack.1 = f32[256,128]{1,0:T(8,128)} custom-call(s32[2,16]{1,0:T(2,128)} %bitcast.33, s32[2]{0:T(128)} %class_ref.3, f32[2,200]{1,0:T(2,128)} %shocks_ref.1), custom_call_target="tpu_custom_call" | custom-call | tf_op jit(solution)/shard_map/pack/pallas_call | solution.py:370
  2.3 15.7 %all-to-all-start = ((f32[256,1,128]{2,1,0:T(1,128)}), f32[256,1,128]{2,1,0:T(1,128)S(1)}, u32[]{:S(2)}, u32[]{:S(2)}) async-start(f32[256,1,128]{2,1,0:T(1,128)} %bitcast.29), calls=%async_computation | async-start | bytes 262144 | tf_op jit(solution)/shard_map/all_to_all | solution.py:483
  18.0 0.7 convert_element_type.16
  18.6 5.6 %path_windows.1 = (f32[4096,128]{1,0:T(8,128)}, s32[16,128]{1,0:T(8,128)}, f32[16,128]{1,0:T(8,128)}) custom-call(s32[16]{0:T(128)} %offsets_ref.1, s32[2,16]{1,0:T(2,128)} %bitcast.34, s32[2]{0:T(128)} %class_ref.3, s32[16]{0:T(128)} %knock_ref.1, s32[16]{0:T(128)} %call_ref.1, s32[16]{0:T(128)} %kind_ref.1, f32[16]{0:T(128)} %book_ref.1, f32[64,2048]{1,0:T(8,128)} %table_ref.1), custom_call_target="tpu_custom_call" | custom-call | tf_op jit(solution)/shard_map/path_windows/pallas_call | solution.py:132
  24.3 6.8 %all-to-all-done = f32[256,1,128]{2,1,0:T(1,128)S(1)} async-done(((f32[256,1,128]{2,1,0:T(1,128)}), f32[256,1,128]{2,1,0:T(1,128)S(1)}, u32[]{:S(2)}, u32[]{:S(2)}) %all-to-all-start) | async-done | bytes 131104 | tf_op jit(solution)/shard_map/all_to_all | solution.py:483
  31.1 0.0 copy-start.1
  31.1 0.6 copy-done.1
  31.7 1.6 %unpack.1 = bf16[32,200]{1,0:T(8,128)(2,1)} custom-call(f32[256,128]{1,0:T(8,128)} %bitcast.26), custom_call_target="tpu_custom_call" | custom-call | tf_op jit(solution)/shard_map/unpack/pallas_call | solution.py:402
  33.4 0.0 copy-done
  33.4 1.1 %fusion.1 = bf16[2,32,1024]{2,1,0:T(8,128)(2,1)S(1)} fusion(bf16[200,2,1024]{2,1,0:T(2,128)(2,1)S(1)} %copy-done, f32[2,1024]{1,0:T(2,128)S(1)} %convert_element_type.16, bf16[32,200]{1,0:T(8,128)(2,1)} %unpack.1), kind=kOutput, calls=%fused_computation.3 | convolution fusion | flops 26345472 | bytes 971264 | tf_op jit(solution)/shard_map/sf,fum->usm/dot_general | solution.py:485
  34.5 0.8 copy.30
  35.3 3.5 %all-to-all-start.1 = ((bf16[2,32,1024]{2,0,1:T(2,128)(2,1)}), bf16[2,32,1024]{2,0,1:T(2,128)(2,1)S(1)}, u32[]{:S(2)}, u32[]{:S(2)}) async-start(bf16[2,32,1024]{2,0,1:T(2,128)(2,1)} %copy.30), calls=%async_computation.1 | async-start | bytes 262144 | tf_op jit(solution)/shard_map/all_to_all | solution.py:492
  38.8 1.0 %slice_convert_fusion = s32[256,2]{1,0:T(8,128)S(1)} fusion(f32[256,128]{1,0:T(8,128)} %bitcast.27), kind=kLoop, calls=%fused_computation.6 | loop fusion | flops 512 | bytes 4096 | tf_op jit(solution)/shard_map/convert_element_type | solution.py:496
  39.8 0.1 reshape.96
  39.9 0.3 convert_reduce_fusion
  40.3 0.1 select_reduce_fusion
  40.5 0.1 copy.32
  40.5 0.1 reshape.99
  40.6 3.9 %path_draws.2.refs_1_ = f32[64,128,128]{2,1,0:T(8,128)} custom-call(f32[4096,128]{1,0:T(8,128)} %get-tuple-element.18.refs_0_), custom_call_target="tpu_custom_call" | custom-call | tf_op jit(solution)/shard_map/path_draws/pallas_call | solution.py:171
  44.5 1.6 %all-to-all-done.1 = bf16[2,32,1024]{2,0,1:T(2,128)(2,1)S(1)} async-done(((bf16[2,32,1024]{2,0,1:T(2,128)(2,1)}), bf16[2,32,1024]{2,0,1:T(2,128)(2,1)S(1)}, u32[]{:S(2)}, u32[]{:S(2)}) %all-to-all-start.1) | async-done | bytes 131104 | tf_op jit(solution)/shard_map/all_to_all | solution.py:492
  46.2 0.1 copy.31
  46.3 0.7 gather_fusion
  47.0 0.8 reshape.98
  47.8 6.7 %all-to-all-start.2 = ((bf16[16,4,2048]{2,1,0:T(4,128)(2,1)}), bf16[16,4,2048]{2,1,0:T(4,128)(2,1)S(1)}, u32[]{:S(2)}, u32[]{:S(2)}) async-start(bf16[16,4,2048]{2,1,0:T(4,128)(2,1)} %reshape.98), calls=%async_computation.2 | async-start | bytes 524288 | tf_op jit(solution)/shard_map/all_to_all | solution.py:508
  54.6 3.9 %path_draws.3.draws_ref = f32[64,128,128]{2,1,0:T(8,128)} custom-call(f32[4096,128]{1,0:T(8,128)} %get-tuple-element.18.refs_0_, f32[64,128,128]{2,1,0:T(8,128)} %path_draws.2.refs_1_), custom_call_target="tpu_custom_call", output_to_operand_aliasing={{}: (1, {})} | custom-call | tf_op jit(solution)/shard_map/path_draws/pallas_call | solution.py:171
  58.5 4.8 %all-to-all-done.2.rows_ref = bf16[16,4,2048]{2,1,0:T(4,128)(2,1)S(1)} async-done(((bf16[16,4,2048]{2,1,0:T(4,128)(2,1)}), bf16[16,4,2048]{2,1,0:T(4,128)(2,1)S(1)}, u32[]{:S(2)}, u32[]{:S(2)}) %all-to-all-start.2) | async-done | bytes 262176 | tf_op jit(solution)/shard_map/all_to_all | solution.py:508
  63.3 0.0 copy-start.2
  63.3 0.7 copy-done.2
  64.0 10.8 %path_values.1 = (f32[2,16]{1,0:T(2,128)}, f32[256,128]{1,0:T(8,128)}) custom-call(bf16[16,4,2048]{2,1,0:T(4,128)(2,1)} %copy-done.2, bf16[256,256]{1,0:T(8,128)(2,1)} %constant.38.clone.basis_ref, s32[16,128]{1,0:T(8,128)} %get-tuple-element.20.terms_ref, f32[16,128]{1,0:T(8,128)} %get-tuple-element.21.book_ref, f32[64,128,128]{2,1,0:T(8,128)} %path_draws.3.draws_ref), custom_call_target="tpu_custom_call" | custom-call | tf_op jit(solution)/shard_map/path_values/pallas_call | solution.py:321
  74.8 21.1 %all_to_all.42 = f32[256,1,128]{2,1,0:T(1,128)} all-to-all(f32[256,1,128]{2,1,0:T(1,128)} %bitcast.32), channel_id=1, replica_groups=mesh['trade'=16,'scen'=16] {'trade','scen'}, dimensions={0} | all-to-all | bytes 262144 | tf_op jit(solution)/shard_map/all_to_all | solution.py:512
  95.9 1.7 %tail.1 = (f32[2]{0:T(128)}, f32[1]{0:T(128)}) custom-call(f32[256,128]{1,0:T(8,128)} %bitcast.30), custom_call_target="tpu_custom_call" | custom-call | tf_op jit(solution)/shard_map/tail/pallas_call | solution.py:442
  (6 shorter events, 0.1 us)
Async XLA Ops:
  0.6 32.7 %copy-start = (bf16[200,2,1024]{2,1,0:T(2,128)(2,1)S(1)}, bf16[200,2,1024]{2,1,0:T(2,128)(2,1)}, u32[]{:S(2)}) copy-start(bf16[200,2,1024]{2,1,0:T(2,128)(2,1)} %param.12) | copy-start | bytes 2457604
  2.3 28.8 %all-to-all-start = ((f32[256,1,128]{2,1,0:T(1,128)}), f32[256,1,128]{2,1,0:T(1,128)S(1)}, u32[]{:S(2)}, u32[]{:S(2)}) async-start(f32[256,1,128]{2,1,0:T(1,128)} %bitcast.29), calls=%async_computation | async-start | bytes 262144 | tf_op jit(solution)/shard_map/all_to_all | solution.py:483
  31.1 0.6 copy-start.1
  35.3 10.9 %all-to-all-start.1 = ((bf16[2,32,1024]{2,0,1:T(2,128)(2,1)}), bf16[2,32,1024]{2,0,1:T(2,128)(2,1)S(1)}, u32[]{:S(2)}, u32[]{:S(2)}) async-start(bf16[2,32,1024]{2,0,1:T(2,128)(2,1)} %copy.30), calls=%async_computation.1 | async-start | bytes 262144 | tf_op jit(solution)/shard_map/all_to_all | solution.py:492
  47.8 15.4 %all-to-all-start.2 = ((bf16[16,4,2048]{2,1,0:T(4,128)(2,1)}), bf16[16,4,2048]{2,1,0:T(4,128)(2,1)S(1)}, u32[]{:S(2)}, u32[]{:S(2)}) async-start(bf16[16,4,2048]{2,1,0:T(4,128)(2,1)} %reshape.98), calls=%async_computation.2 | async-start | bytes 524288 | tf_op jit(solution)/shard_map/all_to_all | solution.py:508
  63.3 0.7 copy-start.2

commit v6 on v5

--- a/solution.py
+++ b/solution.py
@@ -313,7 +313,7 @@
         sent_ref[...] = jnp.broadcast_to(sent[0:1, :], sent_ref.shape)
 
 
-UNROLL = 8
+UNROLL = 16
 
 
 def path_values(rows, terms, book, draws, trades, devices):

time: 98.3 us -> 99 us (level)
  no operation moved by 1% of the time
where the time goes in v6:
time: 99 us; the launch traced here: 98.4 us
  Pallas kernels  29.9 us (30%)
  starting transfers between devices  25.9 us (26%)
  blocking collectives  21.1 us (21%)
  waiting for transfers between devices  13.3 us (13%)
  local copies, waits for them, and re-layouts  4.13 us (4%)
  other arithmetic  2.24 us (2%)
  matrix products  1.08 us (1%)
    all_to_all x1, blocking collectives, per_device(): lax.all_to_all(parts, everywhere, split_axis=0, concat_axis=0, tiled=True)  21.1 us
    all_to_all x1, starting transfers between devices, per_device(): lax.all_to_all(sent, everywhere, split_axis=0, concat_axis=0, tiled=True)  15.7 us
    pallas_call x1, Pallas kernels, path_values(): pl.pallas_call(paths_kernel, grid=(MAT // BLOCK,), out_shape=(jax.ShapeDt...  11.5 us
    pallas_call x2, Pallas kernels, path_draws(): pl.pallas_call(lambda *refs: turn_kernel(half * (MAT // 2), *refs), grid=...  7.77 us
    all_to_all x1, waiting for transfers between devices, per_device(): lax.all_to_all(sent, everywhere, split_axis=0, concat_axis=0, tiled=True)  6.83 us
    all_to_all x1, starting transfers between devices, per_device(): lax.all_to_all(fetched, 'trade', split_axis=0, concat_axis=0, tiled=True)  6.73 us
    pallas_call x1, Pallas kernels, path_windows(): pl.pallas_call(functools.partial(windows_kernel, owned_rows=owned_rows, c...  5.6 us
    all_to_all x1, waiting for transfers between devices, per_device(): lax.all_to_all(fetched, 'trade', split_axis=0, concat_axis=0, tiled=True)  4.79 us
  transfers between devices with their start and end apart: 3, of which 3 were waited for; matrix products, arithmetic and copies ran while one was open for 3% of the time, Pallas kernels for 14%

profile of v6, /device:TPU:1, one launch (start us, length us, event | category | flops | bytes accessed | tf_op | source)
XLA Modules:
  0.0 98.4 jit_solution(927182344427374522)
XLA Ops:
  0.6 0.0 copy-start
  0.6 1.6 %pack.1 = f32[256,128]{1,0:T(8,128)} custom-call(s32[2,16]{1,0:T(2,128)} %bitcast.33, s32[2]{0:T(128)} %class_ref.3, f32[2,200]{1,0:T(2,128)} %shocks_ref.1), custom_call_target="tpu_custom_call" | custom-call | tf_op jit(solution)/shard_map/pack/pallas_call | solution.py:370
  2.3 15.7 %all-to-all-start = ((f32[256,1,128]{2,1,0:T(1,128)}), f32[256,1,128]{2,1,0:T(1,128)S(1)}, u32[]{:S(2)}, u32[]{:S(2)}) async-start(f32[256,1,128]{2,1,0:T(1,128)} %bitcast.29), calls=%async_computation | async-start | bytes 262144 | tf_op jit(solution)/shard_map/all_to_all | solution.py:483
  18.0 0.7 convert_element_type.16
  18.6 5.6 %path_windows.1 = (f32[4096,128]{1,0:T(8,128)}, s32[16,128]{1,0:T(8,128)}, f32[16,128]{1,0:T(8,128)}) custom-call(s32[16]{0:T(128)} %offsets_ref.1, s32[2,16]{1,0:T(2,128)} %bitcast.34, s32[2]{0:T(128)} %class_ref.3, s32[16]{0:T(128)} %knock_ref.1, s32[16]{0:T(128)} %call_ref.1, s32[16]{0:T(128)} %kind_ref.1, f32[16]{0:T(128)} %book_ref.1, f32[64,2048]{1,0:T(8,128)} %table_ref.1), custom_call_target="tpu_custom_call" | custom-call | tf_op jit(solution)/shard_map/path_windows/pallas_call | solution.py:132
  24.3 6.8 %all-to-all-done = f32[256,1,128]{2,1,0:T(1,128)S(1)} async-done(((f32[256,1,128]{2,1,0:T(1,128)}), f32[256,1,128]{2,1,0:T(1,128)S(1)}, u32[]{:S(2)}, u32[]{:S(2)}) %all-to-all-start) | async-done | bytes 131104 | tf_op jit(solution)/shard_map/all_to_all | solution.py:483
  31.1 0.0 copy-start.1
  31.1 0.6 copy-done.1
  31.7 1.6 %unpack.1 = bf16[32,200]{1,0:T(8,128)(2,1)} custom-call(f32[256,128]{1,0:T(8,128)} %bitcast.26), custom_call_target="tpu_custom_call" | custom-call | tf_op jit(solution)/shard_map/unpack/pallas_call | solution.py:402
  33.4 0.0 copy-done
  33.4 1.1 %fusion.1 = bf16[2,32,1024]{2,1,0:T(8,128)(2,1)S(1)} fusion(bf16[200,2,1024]{2,1,0:T(2,128)(2,1)S(1)} %copy-done, f32[2,1024]{1,0:T(2,128)S(1)} %convert_element_type.16, bf16[32,200]{1,0:T(8,128)(2,1)} %unpack.1), kind=kOutput, calls=%fused_computation.3 | convolution fusion | flops 26345472 | bytes 971264 | tf_op jit(solution)/shard_map/sf,fum->usm/dot_general | solution.py:485
  34.5 0.8 copy.30
  35.3 3.5 %all-to-all-start.1 = ((bf16[2,32,1024]{2,0,1:T(2,128)(2,1)}), bf16[2,32,1024]{2,0,1:T(2,128)(2,1)S(1)}, u32[]{:S(2)}, u32[]{:S(2)}) async-start(bf16[2,32,1024]{2,0,1:T(2,128)(2,1)} %copy.30), calls=%async_computation.1 | async-start | bytes 262144 | tf_op jit(solution)/shard_map/all_to_all | solution.py:492
  38.8 1.0 %slice_convert_fusion = s32[256,2]{1,0:T(8,128)S(1)} fusion(f32[256,128]{1,0:T(8,128)} %bitcast.27), kind=kLoop, calls=%fused_computation.6 | loop fusion | flops 512 | bytes 4096 | tf_op jit(solution)/shard_map/convert_element_type | solution.py:496
  39.8 0.1 reshape.96
  39.9 0.3 convert_reduce_fusion
  40.3 0.1 select_reduce_fusion
  40.5 0.1 copy.32
  40.5 0.1 reshape.99
  40.6 3.9 %path_draws.2.refs_1_ = f32[64,128,128]{2,1,0:T(8,128)} custom-call(f32[4096,128]{1,0:T(8,128)} %get-tuple-element.18.refs_0_), custom_call_target="tpu_custom_call" | custom-call | tf_op jit(solution)/shard_map/path_draws/pallas_call | solution.py:171
  44.5 1.6 %all-to-all-done.1 = bf16[2,32,1024]{2,0,1:T(2,128)(2,1)S(1)} async-done(((bf16[2,32,1024]{2,0,1:T(2,128)(2,1)}), bf16[2,32,1024]{2,0,1:T(2,128)(2,1)S(1)}, u32[]{:S(2)}, u32[]{:S(2)}) %all-to-all-start.1) | async-done | bytes 131104 | tf_op jit(solution)/shard_map/all_to_all | solution.py:492
  46.2 0.1 copy.31
  46.3 0.7 gather_fusion
  47.0 0.8 reshape.98
  47.8 6.7 %all-to-all-start.2 = ((bf16[16,4,2048]{2,1,0:T(4,128)(2,1)}), bf16[16,4,2048]{2,1,0:T(4,128)(2,1)S(1)}, u32[]{:S(2)}, u32[]{:S(2)}) async-start(bf16[16,4,2048]{2,1,0:T(4,128)(2,1)} %reshape.98), calls=%async_computation.2 | async-start | bytes 524288 | tf_op jit(solution)/shard_map/all_to_all | solution.py:508
  54.6 3.9 %path_draws.3.draws_ref = f32[64,128,128]{2,1,0:T(8,128)} custom-call(f32[4096,128]{1,0:T(8,128)} %get-tuple-element.18.refs_0_, f32[64,128,128]{2,1,0:T(8,128)} %path_draws.2.refs_1_), custom_call_target="tpu_custom_call", output_to_operand_aliasing={{}: (1, {})} | custom-call | tf_op jit(solution)/shard_map/path_draws/pallas_call | solution.py:171
  58.5 4.8 %all-to-all-done.2.rows_ref = bf16[16,4,2048]{2,1,0:T(4,128)(2,1)S(1)} async-done(((bf16[16,4,2048]{2,1,0:T(4,128)(2,1)}), bf16[16,4,2048]{2,1,0:T(4,128)(2,1)S(1)}, u32[]{:S(2)}, u32[]{:S(2)}) %all-to-all-start.2) | async-done | bytes 262176 | tf_op jit(solution)/shard_map/all_to_all | solution.py:508
  63.3 0.0 copy-start.2
  63.3 0.7 copy-done.2
  64.0 11.5 %path_values.1 = (f32[2,16]{1,0:T(2,128)}, f32[256,128]{1,0:T(8,128)}) custom-call(bf16[16,4,2048]{2,1,0:T(4,128)(2,1)} %copy-done.2, bf16[256,256]{1,0:T(8,128)(2,1)} %constant.38.clone.basis_ref, s32[16,128]{1,0:T(8,128)} %get-tuple-element.20.terms_ref, f32[16,128]{1,0:T(8,128)} %get-tuple-element.21.book_ref, f32[64,128,128]{2,1,0:T(8,128)} %path_draws.3.draws_ref), custom_call_target="tpu_custom_call" | custom-call | tf_op jit(solution)/shard_map/path_values/pallas_call | solution.py:321
  75.5 21.1 %all_to_all.42 = f32[256,1,128]{2,1,0:T(1,128)} all-to-all(f32[256,1,128]{2,1,0:T(1,128)} %bitcast.32), channel_id=1, replica_groups=mesh['trade'=16,'scen'=16] {'trade','scen'}, dimensions={0} | all-to-all | bytes 262144 | tf_op jit(solution)/shard_map/all_to_all | solution.py:512
  96.7 1.7 %tail.1 = (f32[2]{0:T(128)}, f32[1]{0:T(128)}) custom-call(f32[256,128]{1,0:T(8,128)} %bitcast.30), custom_call_target="tpu_custom_call" | custom-call | tf_op jit(solution)/shard_map/tail/pallas_call | solution.py:442
  (6 shorter events, 0.1 us)
Async XLA Ops:
  0.6 32.7 %copy-start = (bf16[200,2,1024]{2,1,0:T(2,128)(2,1)S(1)}, bf16[200,2,1024]{2,1,0:T(2,128)(2,1)}, u32[]{:S(2)}) copy-start(bf16[200,2,1024]{2,1,0:T(2,128)(2,1)} %param.12) | copy-start | bytes 2457604
  2.3 28.8 %all-to-all-start = ((f32[256,1,128]{2,1,0:T(1,128)}), f32[256,1,128]{2,1,0:T(1,128)S(1)}, u32[]{:S(2)}, u32[]{:S(2)}) async-start(f32[256,1,128]{2,1,0:T(1,128)} %bitcast.29), calls=%async_computation | async-start | bytes 262144 | tf_op jit(solution)/shard_map/all_to_all | solution.py:483
  31.1 0.6 copy-start.1
  35.3 10.9 %all-to-all-start.1 = ((bf16[2,32,1024]{2,0,1:T(2,128)(2,1)}), bf16[2,32,1024]{2,0,1:T(2,128)(2,1)S(1)}, u32[]{:S(2)}, u32[]{:S(2)}) async-start(bf16[2,32,1024]{2,0,1:T(2,128)(2,1)} %copy.30), calls=%async_computation.1 | async-start | bytes 262144 | tf_op jit(solution)/shard_map/all_to_all | solution.py:492
  47.8 15.4 %all-to-all-start.2 = ((bf16[16,4,2048]{2,1,0:T(4,128)(2,1)}), bf16[16,4,2048]{2,1,0:T(4,128)(2,1)S(1)}, u32[]{:S(2)}, u32[]{:S(2)}) async-start(bf16[16,4,2048]{2,1,0:T(4,128)(2,1)} %reshape.98), calls=%async_computation.2 | async-start | bytes 524288 | tf_op jit(solution)/shard_map/all_to_all | solution.py:508
  63.3 0.7 copy-start.2
